TPU v7x, 128 devices: a whole 4x4x4 slice. The times are simulated.
128 devices in a mesh: rowk: 8 (over y_hi, z), colk: 16 (over y_lo, x, core).
Axes of the slice: x: 4, y: 4 (y_hi: 2, y_lo: 2; y = y_hi * 2 + y_lo), z: 4, core: 2. Of those that a mesh axis runs over, the one named last changes fastest.
Arguments:
- coarse_kernel: bfloat16 [128, 128, 128, 128], P(('rowk', 'colk')), may hold values from -0.0234375 to 0.0234375
- left_rotation: bfloat16 [256, 2, 128, 128], P('rowk'), may hold values from -0.5 to 0.5
- right_rotation: bfloat16 [256, 2, 128, 128], P('colk'), may hold values from -0.5 to 0.5
- fine_map: int32 [256], replicated, may hold values from 0 to 127, as said below
- coefficient_index: int32 [256, 256, 4], P('rowk', 'colk'), may hold values from 0 to 15, as said below
- coefficient_table: float32 [16], replicated, may hold values from 0.3 to 1
- trial_vectors: bfloat16 [64, 32768], P(None, 'colk'), may hold values from -6 to 6
Outputs:
- forward_image: bfloat16 [64, 32768], P(None, ('rowk', 'colk'))
- adjoint_image: bfloat16 [64, 32768], P('rowk', 'colk')
Inputs may be any that keep to these rules, and one draw needn't show every extreme that they name: `fine_map`: entry i is i // 2 or i // 2 - 1 and lies in the same aligned group of 8 coarse points as i // 2; it equals i // 2 where i // 2 is the first or the last of its group. `coefficient_index`: 0 marks an absent source; slot 0 is never 0.
All inputs are finite; a program needn't handle non-finite values.
Results may differ from a plain program's by a relative error of at most 0.018.
Values may be sent and summed in bfloat16 or wider, within the bound.
No kernel may reach another device: no remote copies, remote signals or barrier semaphores. Data moves between devices by JAX's collectives and lax.ppermute only.
A program may use at most 128 MiB of HBM per device.

v0:
```python
import jax
import jax.numpy as jnp
from jax import lax
from jax.sharding import PartitionSpec as P


def shifted(value, axis, steps):
    count = lax.axis_size(axis)
    pairs = [(source, (source + steps) % count) for source in range(count)]
    return lax.ppermute(value, axis, pairs)


def finish_rows(gathered, weight_block, rotor_block):
    weight_turn = weight_block.transpose(0, 2, 1, 3)
    mixed = (
        weight_turn[:, :, :, 0, None, None] * gathered[:, :, :, 0]
        + weight_turn[:, :, :, 1, None, None] * gathered[:, :, :, 1]
    )
    mixed = mixed.astype(jnp.bfloat16)
    return jnp.einsum(
        "ipba,ipjbc->ijac", rotor_block, mixed, preferred_element_type=jnp.float32
    ).astype(jnp.bfloat16)


def body(
    coarse_kernel,
    left_rotation,
    right_rotation,
    fine_map,
    coefficient_index,
    coefficient_table,
    trial_vectors,
):
    n_rows = lax.axis_size("rowk")
    n_cols = lax.axis_size("colk")
    row_id = lax.axis_index("rowk")
    col_id = lax.axis_index("colk")
    coarse_total = coarse_kernel.shape[1]
    fine_rows = left_rotation.shape[0]
    fine_cols = right_rotation.shape[0]
    band_pairs = left_rotation.shape[2]
    vec_count = trial_vectors.shape[0]
    coarse_rows = coarse_total // n_rows
    coarse_cols = coarse_total // n_cols
    blocks = lax.all_to_all(coarse_kernel, "colk", split_axis=1, concat_axis=0, tiled=True)
    rim_row = shifted(blocks[0:1], "rowk", -1)
    taller = jnp.concatenate([blocks, rim_row], axis=0)
    rim_col = shifted(taller[:, 0:1], "colk", -1)
    local_blocks = jnp.concatenate([taller, rim_col], axis=1)
    offsets = jnp.arange(2, dtype=jnp.int32)
    row_base = (
        lax.dynamic_slice_in_dim(fine_map, row_id * fine_rows, fine_rows) - row_id * coarse_rows
    )
    col_base = (
        lax.dynamic_slice_in_dim(fine_map, col_id * fine_cols, fine_cols) - col_id * coarse_cols
    )
    row_source = row_base[:, None] + offsets[None, :]
    col_source = col_base[:, None] + offsets[None, :]
    entries = jnp.arange(coefficient_table.shape[0], dtype=jnp.int32)
    match = coefficient_index[..., None] == entries
    looked = jnp.sum(
        jnp.where(match, coefficient_table, jnp.zeros_like(coefficient_table)), axis=-1
    )
    weight = jnp.where(coefficient_index > 0, looked, jnp.zeros_like(looked))
    weight = weight.reshape(fine_rows, fine_cols, 2, 2)
    block_rows = 4
    block_count = fine_rows // block_rows
    row_blocks = row_source.reshape(block_count, block_rows, 2)
    weight_blocks = weight.reshape(block_count, block_rows, fine_cols, 2, 2)
    rotor_blocks = left_rotation.reshape(block_count, block_rows, 2, band_pairs, band_pairs)

    def build_rows(pieces):
        sources, weight_block, rotor_block = pieces
        picked = local_blocks[sources[:, :, None, None], col_source[None, None, :, :]]
        rotated = jnp.einsum(
            "ipjqab,jqbc->ipjqac", picked, right_rotation, preferred_element_type=jnp.float32
        ).astype(jnp.bfloat16)
        return finish_rows(rotated, weight_block, rotor_block)

    kernel = lax.map(build_rows, (row_blocks, weight_blocks, rotor_blocks))
    kernel = kernel.reshape(fine_rows, fine_cols, band_pairs, band_pairs)
    vec_cols = trial_vectors.reshape(vec_count, fine_cols, band_pairs)
    partial_value = jnp.einsum(
        "ijac,vjc->via", kernel, vec_cols, preferred_element_type=jnp.float32
    )
    partial_value = partial_value.reshape(vec_count, fine_rows * band_pairs)
    forward_image = lax.psum_scatter(
        partial_value.astype(jnp.bfloat16), "colk", scatter_dimension=1, tiled=True
    )
    row_image = lax.all_gather(forward_image, "colk", axis=1, tiled=True)
    row_three = row_image.reshape(vec_count, fine_rows, band_pairs)
    terms = jnp.einsum("ijac,via->vjc", kernel, row_three, preferred_element_type=jnp.float32)
    adjoint_image = lax.psum_scatter(
        terms.reshape(vec_count // n_rows * lax.axis_size("rowk"), fine_cols * band_pairs).astype(
            jnp.bfloat16
        ),
        "rowk",
        scatter_dimension=0,
        tiled=True,
    )
    return (forward_image, adjoint_image)


def solution(mesh):
    return jax.shard_map(
        body,
        mesh=mesh,
        in_specs=(
            P(("rowk", "colk"), None, None, None),
            P("rowk", None, None, None),
            P("colk", None, None, None),
            P(),
            P("rowk", "colk", None),
            P(),
            P(None, "colk"),
        ),
        out_specs=(P(None, ("rowk", "colk")), P("rowk", "colk")),
        check_vma=False,
    )
```

profile of v0, /device:TPU:0, one launch (start us, length us, event | category | flops | bytes accessed | tf_op | source)
XLA Modules:
  0.0 505.6 jit_solution(6604542358028095039)
XLA Ops:
  7.3 55.8 %all_to_all.12 = bf16[1,128,128,128]{3,2,0,1:T(8,128)(2,1)S(1)} all-to-all(bf16[1,128,128,128]{3,2,0,1:T(8,128)(2,1)} %bitcast.131), channel_id=1, replica_groups=mesh['rowk'=8,'colk'=16] {'colk'}, dimensions={1} | all-to-all | bytes 8388608 | tf_op jit(solution)/shard_map/all_to_all | solution.py:45
  63.1 1.9 copy-done.1
  65.0 6.4 %collective-permute-start = (bf16[1,8,128,128]{3,2,0,1:T(8,128)(2,1)S(1)}, bf16[1,8,128,128]{3,2,0,1:T(8,128)(2,1)S(1)}, u32[]{:S(2)}, u32[]{:S(2)}) collective-permute-start(bf16[1,8,128,128]{3,2,0,1:T(8,128)(2,1)S(1)} %slice.31), channel_id=1, source_target_pairs={{0,112},{16,0},{32,16},{48,32},{64,48},{80,64},{96,80},{112,96},{1... | collective-permute-start | bytes 786440 | tf_op jit(solution)/shard_map/ppermute | solution.py:10
  71.6 0.2 select_reduce_fusion
  71.9 4.4 collective-permute-done
  76.3 1.1 pad_maximum_fusion.1
  77.4 0.1 collective-permute-start.1
  77.7 6.9 %collective-permute-done.1 = bf16[17,1,128,128]{3,2,1,0:T(8,128)(2,1)S(1)} collective-permute-done((bf16[17,1,128,128]{3,2,1,0:T(8,128)(2,1)S(1)}, bf16[17,1,128,128]{3,2,1,0:T(8,128)(2,1)S(1)}, u32[]{:S(2)}, u32[]{:S(2)}) %collective-permute-start.1) | collective-permute-done | bytes 557088 | tf_op jit(solution)/shard_map/ppermute | solution.py:10
  84.6 5.1 %pad_maximum_fusion = bf16[17,9,128,128]{3,2,1,0:T(8,128)(2,1)} fusion(bf16[17,1,128,128]{3,2,1,0:T(8,128)(2,1)S(1)} %collective-permute-done.1, bf16[1,8,128,128]{3,2,1,0:T(8,128)(2,1)S(1)} %bitcast.134, bf16[16,8,128,128]{3,2,1,0:T(8,128)(2,1)} %bitcast.130), kind=kLoop, calls=%fused_computation.31 | loop fusion | flops 5013504 | bytes 10027008 | tf_op jit(solution)/shard_map/concatenate | solution.py:49
  89.7 235.2 %while.11 = (s32[]{:T(128)}, bf16[8,4,16,128,128]{3,4,2,1,0:T(8,128)(2,1)}, f32[8,4,16,2,2]{2,1,0,4,3:T(4,128)S(1)}, s32[8,4,2]{1,2,0:T(2,128)S(1)}, bf16[17,9,1...) while((s32[]{:T(128)}, ...), condition=%wide.region_2.3_spmd.clone, body=%wide.region_1.2_spmd.clone.sunk | while | flops 1628439040 | bytes 45366852 | solution.py:80
  90.0 0.1 reshape.98
  90.1 11.7 %gather_fusion = bf16[256,128,128]{2,1,0:T(8,128)(2,1)} fusion(bf16[17,9,128,128]{3,2,1,0:T(8,128)(2,1)} %get-tuple-element.181, s32[256]{0:T(256)S(1)} %reshape.98), kind=kCustom, calls=%fused_computation.clone.clone.1 | custom fusion | bytes 16779264 | tf_op jit(solution)/shard_map/while/body/eval_jaxpr/gather | solution.py:74
  101.8 9.0 %convert_bitcast_fusion.2 = bf16[4,2,16,2,128,128]{5,4,1,0,3,2:T(8,128)(2,1)} fusion(bf16[4,2,16,2,128,128]{5,4,3,2,1,0:T(8,128)(2,1)} %bitcast.126, bf16[16,2,128,128]{3,2,1,0:T(8,128)(2,1)S(1)} %get-tuple-element.182), kind=kOutput, calls=%fused_computation.8.clone.1 | convolution fusion | flops 1077936128 | bytes 17825792 | tf_op jit(solution)/shard_map/while/body/eval_jaxpr/ipjqab,jqbc->ipjqac/dot_general | solution.py:75
  111.0 7.6 %fusion.49 = bf16[8,4,16,128,128]{3,4,2,1,0:T(8,128)(2,1)} fusion(bf16[8,4,16,128,128]{3,4,2,1,0:T(8,128)(2,1)} %get-tuple-element.169, s32[]{:T(128)} %get-tuple-element.168, bf16[8,4,2,128,128]{4,3,2,1,0:T(8,128)(2,1)} %get-tuple-element.183, bf16[4,2,16,2,128,128]{5,4,1,0,3,2:T(8,128)(2,1)} %convert_bitcast_fusion.2, f32[4,2,16]{1,0,2:T(4,128)S(1)} %copy.102, ...), kind=kOutput, calls=%fused_computation.15.clone.1 | convolution fusion | flops 550502400 | bytes 10749952 | tf_op jit(solution)/shard_map/while/body/eval_jaxpr/ipba,ipjbc->ijac/dot_general | solution.py:20
  118.9 0.1 reshape.98
  119.0 12.1 %gather_fusion = bf16[256,128,128]{2,1,0:T(8,128)(2,1)} fusion(bf16[17,9,128,128]{3,2,1,0:T(8,128)(2,1)} %get-tuple-element.181, s32[256]{0:T(256)S(1)} %reshape.98), kind=kCustom, calls=%fused_computation.clone.clone.1 | custom fusion | bytes 16779264 | tf_op jit(solution)/shard_map/while/body/eval_jaxpr/gather | solution.py:74
  131.1 9.0 %convert_bitcast_fusion.2 = bf16[4,2,16,2,128,128]{5,4,1,0,3,2:T(8,128)(2,1)} fusion(bf16[4,2,16,2,128,128]{5,4,3,2,1,0:T(8,128)(2,1)} %bitcast.126, bf16[16,2,128,128]{3,2,1,0:T(8,128)(2,1)S(1)} %get-tuple-element.182), kind=kOutput, calls=%fused_computation.8.clone.1 | convolution fusion | flops 1077936128 | bytes 17825792 | tf_op jit(solution)/shard_map/while/body/eval_jaxpr/ipjqab,jqbc->ipjqac/dot_general | solution.py:75
  140.3 7.6 %fusion.49 = bf16[8,4,16,128,128]{3,4,2,1,0:T(8,128)(2,1)} fusion(bf16[8,4,16,128,128]{3,4,2,1,0:T(8,128)(2,1)} %get-tuple-element.169, s32[]{:T(128)} %get-tuple-element.168, bf16[8,4,2,128,128]{4,3,2,1,0:T(8,128)(2,1)} %get-tuple-element.183, bf16[4,2,16,2,128,128]{5,4,1,0,3,2:T(8,128)(2,1)} %convert_bitcast_fusion.2, f32[4,2,16]{1,0,2:T(4,128)S(1)} %copy.102, ...), kind=kOutput, calls=%fused_computation.15.clone.1 | convolution fusion | flops 550502400 | bytes 10749952 | tf_op jit(solution)/shard_map/while/body/eval_jaxpr/ipba,ipjbc->ijac/dot_general | solution.py:20
  148.2 0.1 reshape.98
  148.3 12.5 %gather_fusion = bf16[256,128,128]{2,1,0:T(8,128)(2,1)} fusion(bf16[17,9,128,128]{3,2,1,0:T(8,128)(2,1)} %get-tuple-element.181, s32[256]{0:T(256)S(1)} %reshape.98), kind=kCustom, calls=%fused_computation.clone.clone.1 | custom fusion | bytes 16779264 | tf_op jit(solution)/shard_map/while/body/eval_jaxpr/gather | solution.py:74
  160.8 9.0 %convert_bitcast_fusion.2 = bf16[4,2,16,2,128,128]{5,4,1,0,3,2:T(8,128)(2,1)} fusion(bf16[4,2,16,2,128,128]{5,4,3,2,1,0:T(8,128)(2,1)} %bitcast.126, bf16[16,2,128,128]{3,2,1,0:T(8,128)(2,1)S(1)} %get-tuple-element.182), kind=kOutput, calls=%fused_computation.8.clone.1 | convolution fusion | flops 1077936128 | bytes 17825792 | tf_op jit(solution)/shard_map/while/body/eval_jaxpr/ipjqab,jqbc->ipjqac/dot_general | solution.py:75
  170.0 7.6 %fusion.49 = bf16[8,4,16,128,128]{3,4,2,1,0:T(8,128)(2,1)} fusion(bf16[8,4,16,128,128]{3,4,2,1,0:T(8,128)(2,1)} %get-tuple-element.169, s32[]{:T(128)} %get-tuple-element.168, bf16[8,4,2,128,128]{4,3,2,1,0:T(8,128)(2,1)} %get-tuple-element.183, bf16[4,2,16,2,128,128]{5,4,1,0,3,2:T(8,128)(2,1)} %convert_bitcast_fusion.2, f32[4,2,16]{1,0,2:T(4,128)S(1)} %copy.102, ...), kind=kOutput, calls=%fused_computation.15.clone.1 | convolution fusion | flops 550502400 | bytes 10749952 | tf_op jit(solution)/shard_map/while/body/eval_jaxpr/ipba,ipjbc->ijac/dot_general | solution.py:20
  177.9 0.1 reshape.98
  178.0 12.5 %gather_fusion = bf16[256,128,128]{2,1,0:T(8,128)(2,1)} fusion(bf16[17,9,128,128]{3,2,1,0:T(8,128)(2,1)} %get-tuple-element.181, s32[256]{0:T(256)S(1)} %reshape.98), kind=kCustom, calls=%fused_computation.clone.clone.1 | custom fusion | bytes 16779264 | tf_op jit(solution)/shard_map/while/body/eval_jaxpr/gather | solution.py:74
  190.4 9.0 %convert_bitcast_fusion.2 = bf16[4,2,16,2,128,128]{5,4,1,0,3,2:T(8,128)(2,1)} fusion(bf16[4,2,16,2,128,128]{5,4,3,2,1,0:T(8,128)(2,1)} %bitcast.126, bf16[16,2,128,128]{3,2,1,0:T(8,128)(2,1)S(1)} %get-tuple-element.182), kind=kOutput, calls=%fused_computation.8.clone.1 | convolution fusion | flops 1077936128 | bytes 17825792 | tf_op jit(solution)/shard_map/while/body/eval_jaxpr/ipjqab,jqbc->ipjqac/dot_general | solution.py:75
  199.7 7.6 %fusion.49 = bf16[8,4,16,128,128]{3,4,2,1,0:T(8,128)(2,1)} fusion(bf16[8,4,16,128,128]{3,4,2,1,0:T(8,128)(2,1)} %get-tuple-element.169, s32[]{:T(128)} %get-tuple-element.168, bf16[8,4,2,128,128]{4,3,2,1,0:T(8,128)(2,1)} %get-tuple-element.183, bf16[4,2,16,2,128,128]{5,4,1,0,3,2:T(8,128)(2,1)} %convert_bitcast_fusion.2, f32[4,2,16]{1,0,2:T(4,128)S(1)} %copy.102, ...), kind=kOutput, calls=%fused_computation.15.clone.1 | convolution fusion | flops 550502400 | bytes 10749952 | tf_op jit(solution)/shard_map/while/body/eval_jaxpr/ipba,ipjbc->ijac/dot_general | solution.py:20
  207.6 0.1 reshape.98
  207.7 12.1 %gather_fusion = bf16[256,128,128]{2,1,0:T(8,128)(2,1)} fusion(bf16[17,9,128,128]{3,2,1,0:T(8,128)(2,1)} %get-tuple-element.181, s32[256]{0:T(256)S(1)} %reshape.98), kind=kCustom, calls=%fused_computation.clone.clone.1 | custom fusion | bytes 16779264 | tf_op jit(solution)/shard_map/while/body/eval_jaxpr/gather | solution.py:74
  219.8 9.0 %convert_bitcast_fusion.2 = bf16[4,2,16,2,128,128]{5,4,1,0,3,2:T(8,128)(2,1)} fusion(bf16[4,2,16,2,128,128]{5,4,3,2,1,0:T(8,128)(2,1)} %bitcast.126, bf16[16,2,128,128]{3,2,1,0:T(8,128)(2,1)S(1)} %get-tuple-element.182), kind=kOutput, calls=%fused_computation.8.clone.1 | convolution fusion | flops 1077936128 | bytes 17825792 | tf_op jit(solution)/shard_map/while/body/eval_jaxpr/ipjqab,jqbc->ipjqac/dot_general | solution.py:75
  229.0 7.6 %fusion.49 = bf16[8,4,16,128,128]{3,4,2,1,0:T(8,128)(2,1)} fusion(bf16[8,4,16,128,128]{3,4,2,1,0:T(8,128)(2,1)} %get-tuple-element.169, s32[]{:T(128)} %get-tuple-element.168, bf16[8,4,2,128,128]{4,3,2,1,0:T(8,128)(2,1)} %get-tuple-element.183, bf16[4,2,16,2,128,128]{5,4,1,0,3,2:T(8,128)(2,1)} %convert_bitcast_fusion.2, f32[4,2,16]{1,0,2:T(4,128)S(1)} %copy.102, ...), kind=kOutput, calls=%fused_computation.15.clone.1 | convolution fusion | flops 550502400 | bytes 10749952 | tf_op jit(solution)/shard_map/while/body/eval_jaxpr/ipba,ipjbc->ijac/dot_general | solution.py:20
  236.9 0.1 reshape.98
  237.0 11.7 %gather_fusion = bf16[256,128,128]{2,1,0:T(8,128)(2,1)} fusion(bf16[17,9,128,128]{3,2,1,0:T(8,128)(2,1)} %get-tuple-element.181, s32[256]{0:T(256)S(1)} %reshape.98), kind=kCustom, calls=%fused_computation.clone.clone.1 | custom fusion | bytes 16779264 | tf_op jit(solution)/shard_map/while/body/eval_jaxpr/gather | solution.py:74
  248.7 9.0 %convert_bitcast_fusion.2 = bf16[4,2,16,2,128,128]{5,4,1,0,3,2:T(8,128)(2,1)} fusion(bf16[4,2,16,2,128,128]{5,4,3,2,1,0:T(8,128)(2,1)} %bitcast.126, bf16[16,2,128,128]{3,2,1,0:T(8,128)(2,1)S(1)} %get-tuple-element.182), kind=kOutput, calls=%fused_computation.8.clone.1 | convolution fusion | flops 1077936128 | bytes 17825792 | tf_op jit(solution)/shard_map/while/body/eval_jaxpr/ipjqab,jqbc->ipjqac/dot_general | solution.py:75
  257.9 7.6 %fusion.49 = bf16[8,4,16,128,128]{3,4,2,1,0:T(8,128)(2,1)} fusion(bf16[8,4,16,128,128]{3,4,2,1,0:T(8,128)(2,1)} %get-tuple-element.169, s32[]{:T(128)} %get-tuple-element.168, bf16[8,4,2,128,128]{4,3,2,1,0:T(8,128)(2,1)} %get-tuple-element.183, bf16[4,2,16,2,128,128]{5,4,1,0,3,2:T(8,128)(2,1)} %convert_bitcast_fusion.2, f32[4,2,16]{1,0,2:T(4,128)S(1)} %copy.102, ...), kind=kOutput, calls=%fused_computation.15.clone.1 | convolution fusion | flops 550502400 | bytes 10749952 | tf_op jit(solution)/shard_map/while/body/eval_jaxpr/ipba,ipjbc->ijac/dot_general | solution.py:20
  265.8 0.1 reshape.98
  266.0 12.5 %gather_fusion = bf16[256,128,128]{2,1,0:T(8,128)(2,1)} fusion(bf16[17,9,128,128]{3,2,1,0:T(8,128)(2,1)} %get-tuple-element.181, s32[256]{0:T(256)S(1)} %reshape.98), kind=kCustom, calls=%fused_computation.clone.clone.1 | custom fusion | bytes 16779264 | tf_op jit(solution)/shard_map/while/body/eval_jaxpr/gather | solution.py:74
  278.4 9.0 %convert_bitcast_fusion.2 = bf16[4,2,16,2,128,128]{5,4,1,0,3,2:T(8,128)(2,1)} fusion(bf16[4,2,16,2,128,128]{5,4,3,2,1,0:T(8,128)(2,1)} %bitcast.126, bf16[16,2,128,128]{3,2,1,0:T(8,128)(2,1)S(1)} %get-tuple-element.182), kind=kOutput, calls=%fused_computation.8.clone.1 | convolution fusion | flops 1077936128 | bytes 17825792 | tf_op jit(solution)/shard_map/while/body/eval_jaxpr/ipjqab,jqbc->ipjqac/dot_general | solution.py:75
  287.6 7.6 %fusion.49 = bf16[8,4,16,128,128]{3,4,2,1,0:T(8,128)(2,1)} fusion(bf16[8,4,16,128,128]{3,4,2,1,0:T(8,128)(2,1)} %get-tuple-element.169, s32[]{:T(128)} %get-tuple-element.168, bf16[8,4,2,128,128]{4,3,2,1,0:T(8,128)(2,1)} %get-tuple-element.183, bf16[4,2,16,2,128,128]{5,4,1,0,3,2:T(8,128)(2,1)} %convert_bitcast_fusion.2, f32[4,2,16]{1,0,2:T(4,128)S(1)} %copy.102, ...), kind=kOutput, calls=%fused_computation.15.clone.1 | convolution fusion | flops 550502400 | bytes 10749952 | tf_op jit(solution)/shard_map/while/body/eval_jaxpr/ipba,ipjbc->ijac/dot_general | solution.py:20
  295.5 0.1 reshape.98
  295.6 12.5 %gather_fusion = bf16[256,128,128]{2,1,0:T(8,128)(2,1)} fusion(bf16[17,9,128,128]{3,2,1,0:T(8,128)(2,1)} %get-tuple-element.181, s32[256]{0:T(256)S(1)} %reshape.98), kind=kCustom, calls=%fused_computation.clone.clone.1 | custom fusion | bytes 16779264 | tf_op jit(solution)/shard_map/while/body/eval_jaxpr/gather | solution.py:74
  308.1 9.0 %convert_bitcast_fusion.2 = bf16[4,2,16,2,128,128]{5,4,1,0,3,2:T(8,128)(2,1)} fusion(bf16[4,2,16,2,128,128]{5,4,3,2,1,0:T(8,128)(2,1)} %bitcast.126, bf16[16,2,128,128]{3,2,1,0:T(8,128)(2,1)S(1)} %get-tuple-element.182), kind=kOutput, calls=%fused_computation.8.clone.1 | convolution fusion | flops 1077936128 | bytes 17825792 | tf_op jit(solution)/shard_map/while/body/eval_jaxpr/ipjqab,jqbc->ipjqac/dot_general | solution.py:75
  317.3 7.6 %fusion.49 = bf16[8,4,16,128,128]{3,4,2,1,0:T(8,128)(2,1)} fusion(bf16[8,4,16,128,128]{3,4,2,1,0:T(8,128)(2,1)} %get-tuple-element.169, s32[]{:T(128)} %get-tuple-element.168, bf16[8,4,2,128,128]{4,3,2,1,0:T(8,128)(2,1)} %get-tuple-element.183, bf16[4,2,16,2,128,128]{5,4,1,0,3,2:T(8,128)(2,1)} %convert_bitcast_fusion.2, f32[4,2,16]{1,0,2:T(4,128)S(1)} %copy.102, ...), kind=kOutput, calls=%fused_computation.15.clone.1 | convolution fusion | flops 550502400 | bytes 10749952 | tf_op jit(solution)/shard_map/while/body/eval_jaxpr/ipba,ipjbc->ijac/dot_general | solution.py:20
  324.9 7.4 %fusion.24 = bf16[32,8,8,128]{3,2,1,0:T(8,128)(2,1)S(1)} fusion(bf16[32,16,128,128]{2,3,1,0:T(8,128)(2,1)} %bitcast.127, bf16[64,2048]{1,0:T(8,128)(2,1)S(1)} %copy-done), kind=kOutput, calls=%fused_computation.36 | convolution fusion | flops 1074003968 | bytes 17563648 | tf_op jit(solution)/shard_map/ijac,vjc->via/dot_general | solution.py:83
  332.3 0.9 copy.91
  333.3 65.1 %reduce-scatter.3.cloned.1.call-done = bf16[64,256]{1,0:T(8,128)(2,1)} async-done(((bf16[64,4096]{1,0:T(8,128)(2,1)}), bf16[64,256]{1,0:T(8,128)(2,1)}) %reduce-scatter.3.cloned.1.call-update) | async-done | bytes 32784 | tf_op jit(solution)/shard_map/reduce_scatter | solution.py:87
  398.4 17.9 %all_gather.3 = bf16[64,4096]{1,0:T(8,128)(2,1)S(1)} all-gather(bf16[64,256]{1,0:T(8,128)(2,1)} %reduce-scatter.3.cloned.1.call-done), channel_id=1, replica_groups=mesh['rowk'=8,'colk'=16] {'colk'}, dimensions={1}, use_global_device_ids=true | all-gather | bytes 557056 | tf_op jit(solution)/shard_map/all_gather | solution.py:90
  416.3 11.6 %fusion.22 = bf16[64,2048]{1,0:T(8,128)(2,1)} fusion(bf16[2048,128,32]{1,0,2:T(8,128)(2,1)} %bitcast.128, bf16[64,4096]{1,0:T(8,128)(2,1)S(1)} %all_gather.3), kind=kOutput, calls=%fused_computation.33 | convolution fusion | flops 1073872896 | bytes 17563648 | tf_op jit(solution)/shard_map/ijac,via->vjc/dot_general | solution.py:92
  428.0 70.8 %reduce-scatter.5.cloned.1.call-done = bf16[8,2048]{1,0:T(8,128)(2,1)} async-done(((bf16[64,2048]{1,0:T(8,128)(2,1)}), bf16[8,2048]{1,0:T(8,128)(2,1)}) %reduce-scatter.5.cloned.1.call-update) | async-done | bytes 32784 | tf_op jit(solution)/shard_map/reduce_scatter | solution.py:93
  (95 shorter events, 4.4 us)
Async XLA Ops:
  7.2 317.7 %copy-start = (bf16[64,2048]{1,0:T(8,128)(2,1)S(1)}, bf16[64,2048]{1,0:T(8,128)(2,1)}, u32[]{:S(2)}) copy-start(bf16[64,2048]{1,0:T(8,128)(2,1)} %param.15) | copy-start | bytes 786436
  7.2 64.3 %copy-start.4 = (s32[256]{0:T(256)S(1)}, s32[256]{0:T(256)}, u32[]{:S(2)}) copy-start(s32[256]{0:T(256)} %param.12) | copy-start | bytes 3076
  7.2 64.5 %copy-start.3 = (s32[32,16,4]{0,2,1:T(4,128)S(1)}, s32[32,16,4]{0,2,1:T(4,128)}, u32[]{:S(2)}) copy-start(s32[32,16,4]{0,2,1:T(4,128)} %param.13) | copy-start | bytes 24580
  7.2 64.4 %copy-start.5 = (f32[16]{0:T(128)S(1)}, f32[16]{0:T(128)}, u32[]{:S(2)}) copy-start(f32[16]{0:T(128)} %param.14) | copy-start | bytes 196
  7.2 391.2 %reduce-scatter.3.cloned.1.call-start = ((), (), s32[]{:S(2)}) async-start(), calls=%async_computation.3 | async-start | bytes 557056 | tf_op jit(solution)/shard_map/reduce_scatter | solution.py:87
  63.1 1.9 copy-start.1
  65.0 24.7 %copy-start.2 = (bf16[16,2,128,128]{3,2,1,0:T(8,128)(2,1)S(1)}, bf16[16,2,128,128]{3,2,1,0:T(8,128)(2,1)}, u32[]{:S(2)}) copy-start(bf16[16,2,128,128]{3,2,1,0:T(8,128)(2,1)} %param.11) | copy-start | bytes 3145732
  65.0 11.2 %collective-permute-start = (bf16[1,8,128,128]{3,2,0,1:T(8,128)(2,1)S(1)}, bf16[1,8,128,128]{3,2,0,1:T(8,128)(2,1)S(1)}, u32[]{:S(2)}, u32[]{:S(2)}) collective-permute-start(bf16[1,8,128,128]{3,2,0,1:T(8,128)(2,1)S(1)} %slice.31), channel_id=1, source_target_pairs={{0,112},{16,0},{32,16},{48,32},{64,48},{80,64},{96,80},{112,96},{1... | collective-permute-start | bytes 786440 | tf_op jit(solution)/shard_map/ppermute | solution.py:10
  77.4 7.2 %collective-permute-start.1 = (bf16[17,1,128,128]{3,2,1,0:T(8,128)(2,1)S(1)}, bf16[17,1,128,128]{3,2,1,0:T(8,128)(2,1)S(1)}, u32[]{:S(2)}, u32[]{:S(2)}) collective-permute-start(bf16[17,1,128,128]{3,2,1,0:T(8,128)(2,1)S(1)} %pad_maximum_fusion.1), channel_id=1, source_target_pairs={{0,15},{1,0},{2,1},{3,2},{4,3},{5,4},{6,5},{7,6},{8,7},{9,8},{10,9... | collective-permute-start | bytes 1671176 | tf_op jit(solution)/shard_map/ppermute | solution.py:10
  333.2 165.5 %reduce-scatter.5.cloned.1.call-start = ((), (), s32[]{:S(2)}) async-start(), calls=%async_computation.4 | async-start | bytes 294912 | tf_op jit(solution)/shard_map/reduce_scatter | solution.py:93
Sparse Core Ops, SparseCore 0:
  333.4 64.9 reduce-scatter.2
  428.1 70.5 reduce-scatter.4
where the time goes:
time: 507 us; the launch traced here: 506 us
  matrix products  152 us (30%)
  waiting for transfers between devices  147 us (29%)
  local copies, waits for them, and re-layouts  104 us (21%)
  blocking collectives  73.8 us (15%)
  between operations  14.1 us (3%)
  other arithmetic  7.89 us (2%)
  starting transfers between devices  6.65 us (1%)
    gather x8, local copies, waits for them, and re-layouts, build_rows(): local_blocks[sources[:, :, None, None], col_source[None, None, :, :]]  97.4 us
    dot_general x8, matrix products, build_rows(): jnp.einsum('ipjqab,jqbc->ipjqac', picked, right_rotation, preferred_eleme...  71.8 us
    reduce_scatter x1, waiting for transfers between devices, body(): lax.psum_scatter(terms.reshape(vec_count // n_rows * lax.axis_size('rowk'...  70.8 us
    reduce_scatter x1, waiting for transfers between devices, body(): lax.psum_scatter(partial_value.astype(jnp.bfloat16), 'colk', scatter_dime...  65.1 us
    dot_general x8, matrix products, finish_rows(): jnp.einsum('ipba,ipjbc->ijac', rotor_block, mixed, preferred_element_type...  61 us
    all_to_all x1, blocking collectives, body(): lax.all_to_all(coarse_kernel, 'colk', split_axis=1, concat_axis=0, tiled=...  55.8 us
    all_gather x1, blocking collectives, body(): row_image = lax.all_gather(forward_image, 'colk', axis=1, tiled=True)  17.9 us
    dot_general x1, matrix products, body(): jnp.einsum('ijac,via->vjc', kernel, row_three, preferred_element_type=jnp...  11.6 us
  transfers between devices with their start and end apart: 4, of which 4 were waited for; matrix products, arithmetic and copies ran while one was open for 0% of the time, Pallas kernels for 0%

commit v1 on v0

v1 whole, which is shorter than its diff:
```python
import jax
import jax.numpy as jnp
from jax import lax
from jax.experimental import pallas as pl
from jax.experimental.pallas import tpu as pltpu
from jax.sharding import PartitionSpec as P

VMEM = pl.BlockSpec(memory_space=pltpu.VMEM)
SMEM = pl.BlockSpec(memory_space=pltpu.SMEM)
NT = (((1,), (1,)), ((), ()))


def dot(left, right):
    return jnp.dot(left, right, preferred_element_type=jnp.float32)


def dot_nt(left, right):
    return lax.dot_general(left, right, NT, preferred_element_type=jnp.float32)


def shifted(value, axis, steps):
    count = lax.axis_size(axis)
    pairs = [(source, (source + steps) % count) for source in range(count)]
    return lax.ppermute(value, axis, pairs)


def rotate_kernel(x_ref, right_ref, out_ref):
    fine_cols = right_ref.shape[0]
    nb = right_ref.shape[2]
    for j in range(fine_cols):
        x_now = x_ref[:, j * nb : (j + 1) * nb]
        for dq in range(2):
            out_ref[2 * j + dq] = dot_nt(x_now, right_ref[j, dq]).astype(jnp.bfloat16)


def forward_kernel(
    index_ref, table_ref, rows_ref, cols_ref, u_ref, blocks_ref, rim_row_ref, rim_col_ref, corner_ref, left_ref, out_ref, z_ref
):
    n_p, n_q = blocks_ref.shape[:2]
    n_pairs = u_ref.shape[0]
    fine_cols = n_pairs // 2
    nb = blocks_ref.shape[-1]
    n_dest = out_ref.shape[0]
    own = left_ref.shape[0] // n_dest

    def spread(pair, carry):
        q = cols_ref[pair // 2] + pair % 2
        u_now = u_ref[pair]
        for p in range(n_p):
            z_ref[p, pair] = dot_nt(u_now, blocks_ref[p, q])
        z_ref[n_p, pair] = dot_nt(u_now, rim_row_ref[q])
        return carry

    def spread_rim(pair):
        u_now = u_ref[pair]
        for p in range(n_p):
            z_ref[p, pair] = dot_nt(u_now, rim_col_ref[p])
        z_ref[n_p, pair] = dot_nt(u_now, corner_ref[...])

    lax.fori_loop(0, n_pairs - 3, spread, 0)
    spread(n_pairs - 2, 0)
    spread_rim(n_pairs - 3)
    spread_rim(n_pairs - 1)

    def finish(dest, carry):
        for step in range(own):
            i = dest * own + step
            total = None
            for dp in range(2):
                p = rows_ref[i] + dp
                acc = None
                for pair in range(n_pairs):
                    where = (i * fine_cols + pair // 2) * 4 + 2 * dp + pair % 2
                    term = table_ref[index_ref[where]] * z_ref[p, pair]
                    acc = term if acc is None else acc + term
                part = dot(acc.astype(jnp.bfloat16), left_ref[i, dp])
                total = part if total is None else total + part
            out_ref[dest, :, step * nb : (step + 1) * nb] = total.astype(jnp.bfloat16)
        return carry

    lax.fori_loop(0, n_dest, finish, 0)


def adjoint_kernel(
    index_ref, table_ref, rows_ref, cols_ref, y_ref, blocks_ref, rim_row_ref, rim_col_ref, corner_ref, left_ref, right_ref, out_ref, z_ref
):
    n_p, n_q = blocks_ref.shape[:2]
    fine_rows = left_ref.shape[0]
    fine_cols = right_ref.shape[0]
    nb = blocks_ref.shape[-1]
    n_dest = y_ref.shape[0]
    own = fine_rows // n_dest

    def source(i, dp, y_now):
        return dot_nt(y_now, left_ref[i, dp]).astype(jnp.bfloat16)

    def y_of(dest, step):
        return y_ref[dest, :, step * nb : (step + 1) * nb]

    def spread(dest, carry):
        for step in range(own):
            i = dest * own + step
            y_now = y_of(dest, step)
            for dp in range(2):
                s_now = source(i, dp, y_now)
                p = rows_ref[i] + dp
                for q in range(n_q):
                    z_ref[2 * i + dp, q] = dot(s_now, blocks_ref[p, q])
                z_ref[2 * i + dp, n_q] = dot(s_now, rim_col_ref[p])
        return carry

    lax.fori_loop(0, n_dest - 1, spread, 0)
    dest = n_dest - 1
    for step in range(own):
        i = dest * own + step
        y_now = y_of(dest, step)
        s_now = source(i, 0, y_now)
        for q in range(n_q):
            z_ref[2 * i, q] = dot(s_now, blocks_ref[n_p - 1, q])
        z_ref[2 * i, n_q] = dot(s_now, rim_col_ref[n_p - 1])
        s_now = source(i, 1, y_now)
        for q in range(n_q):
            z_ref[2 * i + 1, q] = dot(s_now, rim_row_ref[q])
        z_ref[2 * i + 1, n_q] = dot(s_now, corner_ref[...])

    for j in range(fine_cols):
        total = None
        for dq in range(2):
            q = cols_ref[j] + dq

            def gather(i, acc):
                for dp in range(2):
                    where = (i * fine_cols + j) * 4 + 2 * dp + dq
                    acc = acc + table_ref[index_ref[where]] * z_ref[2 * i + dp, q]
                return acc

            start = jnp.zeros(z_ref.shape[2:], jnp.float32)
            acc = lax.fori_loop(0, fine_rows, gather, start, unroll=8)
            part = dot(acc.astype(jnp.bfloat16), right_ref[j, dq])
            total = part if total is None else total + part
        out_ref[:, j * nb : (j + 1) * nb] = total.astype(jnp.bfloat16)


def exchange(value, axis):
    return lax.all_to_all(value, axis, split_axis=0, concat_axis=0, tiled=True)


def body(
    coarse_kernel,
    left_rotation,
    right_rotation,
    fine_map,
    coefficient_index,
    coefficient_table,
    trial_vectors,
):
    n_rows = lax.axis_size("rowk")
    n_cols = lax.axis_size("colk")
    row_id = lax.axis_index("rowk")
    col_id = lax.axis_index("colk")
    coarse_total = coarse_kernel.shape[1]
    fine_rows = left_rotation.shape[0]
    fine_cols = right_rotation.shape[0]
    nb = left_rotation.shape[2]
    vecs = trial_vectors.shape[0]
    coarse_rows = coarse_total // n_rows
    coarse_cols = coarse_total // n_cols
    own = fine_rows // n_cols

    blocks = lax.all_to_all(coarse_kernel, "colk", split_axis=1, concat_axis=0, tiled=True)
    rim_row = shifted(blocks[0:1], "rowk", -1)
    rim_col = shifted(jnp.concatenate([blocks[:, 0], rim_row[:, 0]], axis=0), "colk", -1)
    rim_row = rim_row[0]
    corner = rim_col[coarse_rows]

    rows = lax.dynamic_slice_in_dim(fine_map, row_id * fine_rows, fine_rows) - row_id * coarse_rows
    cols = lax.dynamic_slice_in_dim(fine_map, col_id * fine_cols, fine_cols) - col_id * coarse_cols
    index = coefficient_index.reshape(-1)
    entries = jnp.arange(coefficient_table.shape[0], dtype=jnp.int32)
    table = jnp.where(entries > 0, coefficient_table, jnp.zeros_like(coefficient_table))

    u = pl.pallas_call(
        rotate_kernel,
        out_shape=jax.ShapeDtypeStruct((2 * fine_cols, vecs, nb), jnp.bfloat16),
        in_specs=[VMEM, VMEM],
        out_specs=VMEM,
        name="rotate",
    )(trial_vectors, right_rotation)

    partial = pl.pallas_call(
        forward_kernel,
        out_shape=jax.ShapeDtypeStruct((n_cols, vecs, own * nb), jnp.bfloat16),
        in_specs=[SMEM] * 4 + [VMEM] * 6,
        out_specs=VMEM,
        scratch_shapes=[pltpu.VMEM((coarse_rows + 1, 2 * fine_cols, vecs, nb), jnp.float32)],
        name="forward",
    )(index, table, rows, cols, u, blocks, rim_row, rim_col, corner, left_rotation)

    forward_image = jnp.sum(exchange(partial, "colk").astype(jnp.float32), axis=0).astype(jnp.bfloat16)
    copies = lax.optimization_barrier(jnp.broadcast_to(forward_image, (n_cols, vecs, own * nb)))
    row_image = exchange(copies, "colk")

    terms = pl.pallas_call(
        adjoint_kernel,
        out_shape=jax.ShapeDtypeStruct((vecs, fine_cols * nb), jnp.bfloat16),
        in_specs=[SMEM] * 4 + [VMEM] * 7,
        out_specs=VMEM,
        scratch_shapes=[pltpu.VMEM((2 * fine_rows, coarse_cols + 1, vecs, nb), jnp.float32)],
        name="adjoint",
    )(index, table, rows, cols, row_image, blocks, rim_row, rim_col, corner, left_rotation, right_rotation)

    terms = terms.reshape(n_rows, vecs // n_rows, fine_cols * nb)
    adjoint_image = jnp.sum(exchange(terms, "rowk").astype(jnp.float32), axis=0).astype(jnp.bfloat16)
    return (forward_image, adjoint_image)


def solution(mesh):
    return jax.shard_map(
        body,
        mesh=mesh,
        in_specs=(
            P(("rowk", "colk"), None, None, None),
            P("rowk", None, None, None),
            P("colk", None, None, None),
            P(),
            P("rowk", "colk", None),
            P(),
            P(None, "colk"),
        ),
        out_specs=(P(None, ("rowk", "colk")), P("rowk", "colk")),
        check_vma=False,
    )
```

time: 507 us -> 181 us (0.36)
  matrix products: 152 us -> 0 us
  waiting for transfers between devices: 147 us -> 6.2 us
  local copies, waits for them, and re-layouts: 104 us -> 1.91 us
  Pallas kernels: 0 us -> 59.3 us
  blocking collectives: 73.8 us -> 103 us
  between operations: 14.1 us -> 0.69 us
  other arithmetic: 7.89 us -> 2.47 us
    dot_general x18 -> x0, matrix products: 152 us -> none  [the longest x8 71.8 us: build_rows(): jnp.einsum('ipjqab,jqbc->ipjqac', picked, right_rotation, preferred_eleme...]
    reduce_scatter x2 -> x0, waiting for transfers between devices: 136 us -> none  [the longest x1 70.8 us: body(): lax.psum_scatter(terms.reshape(vec_count // n_rows * lax.axis_size('rowk'...]
    gather x8 -> x0, local copies, waits for them, and re-layouts: 97.4 us -> none  [build_rows(): local_blocks[sources[:, :, None, None], col_source[None, None, :, :]]]
    pallas_call x0 -> x3, Pallas kernels: none -> 59.3 us  [the longest x1 29.4 us: body(): pl.pallas_call(adjoint_kernel, out_shape=jax.ShapeDtypeStruct((vecs, fine...]
    all_to_all x0 -> x3, blocking collectives: none -> 47.7 us  [exchange(): return lax.all_to_all(value, axis, split_axis=0, concat_axis=0, tiled=True)]
    all_gather x1 -> x0, blocking collectives: 17.9 us -> none  [body(): row_image = lax.all_gather(forward_image, 'colk', axis=1, tiled=True)]
    concatenate x26 -> x1, other arithmetic: 7.48 us -> 0.05 us  [body(): jnp.concatenate([blocks[:, 0], rim_row[:, 0]], axis=0)]
  transfers between devices with their start and end apart: 4 -> 2, of which waited for: 4 -> 2; matrix products, arithmetic and copies ran while one was open for 0% -> 1% of each run, Pallas kernels for 0% -> 2%
where the time goes in v1:
time: 181 us
  blocking collectives  103 us (57%)
  Pallas kernels  59.3 us (33%)
  starting transfers between devices  6.57 us (4%)
  waiting for transfers between devices  6.2 us (3%)
  other arithmetic  2.47 us (1%)
  local copies, waits for them, and re-layouts  1.91 us (1%)
    all_to_all x1, blocking collectives, body(): lax.all_to_all(coarse_kernel, 'colk', split_axis=1, concat_axis=0, tiled=...  55.7 us
    all_to_all x3, blocking collectives, exchange(): return lax.all_to_all(value, axis, split_axis=0, concat_axis=0, tiled=True)  47.7 us
    pallas_call x1, Pallas kernels, body(): pl.pallas_call(adjoint_kernel, out_shape=jax.ShapeDtypeStruct((vecs, fine...  29.4 us
    pallas_call x1, Pallas kernels, body(): pl.pallas_call(forward_kernel, out_shape=jax.ShapeDtypeStruct((n_cols, ve...  26.9 us
    ppermute x2, starting transfers between devices, shifted(): return lax.ppermute(value, axis, pairs)  6.57 us
    ppermute x2, waiting for transfers between devices, shifted(): return lax.ppermute(value, axis, pairs)  6.2 us
  transfers between devices with their start and end apart: 2, of which 2 were waited for; matrix products, arithmetic and copies ran while one was open for 1% of the time, Pallas kernels for 2%

profile of v1, /device:TPU:0, one launch (start us, length us, event | category | flops | bytes accessed | tf_op | source)
XLA Modules:
  0.0 180.5 jit_solution(5298327147372030172)
XLA Ops:
  0.6 0.0 copy-start.4
  0.6 55.7 %all_to_all.27 = bf16[1,128,128,128]{3,2,0,1:T(8,128)(2,1)S(1)} all-to-all(bf16[1,128,128,128]{3,2,0,1:T(8,128)(2,1)} %bitcast.17), channel_id=1, replica_groups=mesh['rowk'=8,'colk'=16] {'colk'}, dimensions={1} | all-to-all | bytes 8388608 | tf_op jit(solution)/shard_map/all_to_all | solution.py:170
  56.3 0.0 copy-start
  56.3 0.0 copy-start.5
  56.3 0.0 copy-start.6
  56.4 6.4 %collective-permute-start = (bf16[1,8,128,128]{3,2,1,0:T(8,128)(2,1)S(1)}, bf16[1,8,128,128]{3,2,1,0:T(8,128)(2,1)S(1)}, u32[]{:S(2)}, u32[]{:S(2)}) collective-permute-start(bf16[1,8,128,128]{3,2,1,0:T(8,128)(2,1)S(1)} %slice.17), channel_id=1, source_target_pairs={{0,112},{16,0},{32,16},{48,32},{64,48},{80,64},{96,80},{112,96},{1... | collective-permute-start | bytes 786440 | tf_op jit(solution)/shard_map/ppermute | solution.py:24
  62.8 0.0 copy-done
  62.9 4.8 %collective-permute-done = bf16[1,8,128,128]{3,2,1,0:T(8,128)(2,1)S(1)} collective-permute-done((bf16[1,8,128,128]{3,2,1,0:T(8,128)(2,1)S(1)}, bf16[1,8,128,128]{3,2,1,0:T(8,128)(2,1)S(1)}, u32[]{:S(2)}, u32[]{:S(2)}) %collective-permute-start) | collective-permute-done | bytes 262176 | tf_op jit(solution)/shard_map/ppermute | solution.py:24
  67.6 0.0 copy-start.2
  67.6 0.1 pad_maximum_fusion
  67.7 0.1 collective-permute-start.1
  67.8 0.0 copy-done.4
  67.8 0.2 copy.17
  68.0 0.8 reshape.14.index_ref
  68.8 2.9 %rotate.1.u_ref = bf16[32,64,128]{2,1,0:T(8,128)(2,1)} custom-call(bf16[64,2048]{1,0:T(8,128)(2,1)} %x_ref.1, bf16[16,2,128,128]{3,2,1,0:T(8,128)(2,1)} %right_ref.3), custom_call_target="tpu_custom_call" | custom-call | tf_op jit(solution)/shard_map/rotate/pallas_call | solution.py:182
  71.7 0.0 copy-done.5
  71.7 0.6 dynamic-slice_subtract_fusion.cols_ref
  72.3 0.6 dynamic-slice_subtract_fusion.1.rows_ref
  72.9 0.0 copy-done.6
  72.9 0.5 compare_select_fusion.table_ref
  73.4 1.4 collective-permute-done.1.rim_col_ref
  74.8 0.0 copy-start.1
  74.8 0.7 slice_bitcast_fusion.1.corner_ref
  75.5 0.0 copy-done.2
  75.5 0.2 copy-done.1
  75.7 26.9 %forward.1 = bf16[16,64,256]{2,1,0:T(8,128)(2,1)} custom-call(s32[2048]{0:T(1024)} %reshape.14.index_ref, f32[16]{0:T(128)} %compare_select_fusion.table_ref, s32[32]{0:T(128)} %dynamic-slice_subtract_fusion.1.rows_ref, s32[16]{0:T(128)} %dynamic-slice_subtract_fusion.cols_ref, bf16[32,64,128]{2,1,0:T(8,128)(2,1)} %rotate.1.u_ref, ...), custom_call_target="tpu_custom_call" | custom-call | tf_op jit(solution)/shard_map/forward/pallas_call | solution.py:190
  102.6 17.5 %all_to_all.28 = bf16[16,64,256]{2,1,0:T(8,128)(2,1)S(1)} all-to-all(bf16[16,64,256]{2,1,0:T(8,128)(2,1)} %forward.1), channel_id=1, replica_groups=mesh['rowk'=8,'colk'=16] {'colk'}, dimensions={0} | all-to-all | bytes 1048576 | tf_op jit(solution)/shard_map/all_to_all | solution.py:145
  120.1 0.1 reduce_sum.24
  120.2 0.0 copy-start.3
  120.2 14.1 %all_to_all.29.y_ref = bf16[16,64,256]{2,1,0:T(8,128)(2,1)} all-to-all(bf16[16,64,256]{2,1,0:T(8,128)(2,1)S(1)} %broadcast_in_dim.3), channel_id=1, replica_groups=mesh['rowk'=8,'colk'=16] {'colk'}, dimensions={0} | all-to-all | bytes 1048576 | tf_op jit(solution)/shard_map/all_to_all | solution.py:145
  134.3 29.4 %adjoint.1 = bf16[64,2048]{1,0:T(8,128)(2,1)} custom-call(s32[2048]{0:T(1024)} %reshape.14.index_ref, f32[16]{0:T(128)} %compare_select_fusion.table_ref, s32[32]{0:T(128)} %dynamic-slice_subtract_fusion.1.rows_ref, s32[16]{0:T(128)} %dynamic-slice_subtract_fusion.cols_ref, bf16[16,64,256]{2,1,0:T(8,128)(2,1)} %all_to_all.29.y_ref, ...), custom_call_target="tpu_custom_call" | custom-call | tf_op jit(solution)/shard_map/adjoint/pallas_call | solution.py:203
  163.8 0.0 copy-done.3
  163.8 16.1 %all_to_all.30 = bf16[8,8,2048]{2,1,0:T(8,128)(2,1)S(1)} all-to-all(bf16[8,8,2048]{2,1,0:T(8,128)(2,1)} %bitcast.20), channel_id=1, replica_groups=mesh['rowk'=8,'colk'=16] {'rowk'}, dimensions={0} | all-to-all | bytes 524288 | tf_op jit(solution)/shard_map/all_to_all | solution.py:145
  179.9 0.7 reduce_sum.25
  (4 shorter events, 0.1 us)
Async XLA Ops:
  0.6 67.2 %copy-start.4 = (s32[32,16,4]{0,2,1:T(4,128)S(1)}, s32[32,16,4]{0,2,1:T(4,128)}, u32[]{:S(2)}) copy-start(s32[32,16,4]{0,2,1:T(4,128)} %param.11) | copy-start | bytes 24580
  56.3 6.5 %copy-start = (bf16[1,128,128,128]{3,2,0,1:T(8,128)(2,1)}, bf16[1,128,128,128]{3,2,0,1:T(8,128)(2,1)S(1)}, u32[]{:S(2)}) copy-start(bf16[1,128,128,128]{3,2,0,1:T(8,128)(2,1)S(1)} %all_to_all.27) | copy-start | bytes 12582916
  56.3 15.4 %copy-start.5 = (s32[256]{0:T(256)S(1)}, s32[256]{0:T(256)}, u32[]{:S(2)}) copy-start(s32[256]{0:T(256)} %param.10) | copy-start | bytes 3076
  56.3 16.5 %copy-start.6 = (f32[16]{0:T(128)S(1)}, f32[16]{0:T(128)}, u32[]{:S(2)}) copy-start(f32[16]{0:T(128)} %param.12) | copy-start | bytes 196
  56.4 11.2 %collective-permute-start = (bf16[1,8,128,128]{3,2,1,0:T(8,128)(2,1)S(1)}, bf16[1,8,128,128]{3,2,1,0:T(8,128)(2,1)S(1)}, u32[]{:S(2)}, u32[]{:S(2)}) collective-permute-start(bf16[1,8,128,128]{3,2,1,0:T(8,128)(2,1)S(1)} %slice.17), channel_id=1, source_target_pairs={{0,112},{16,0},{32,16},{48,32},{64,48},{80,64},{96,80},{112,96},{1... | collective-permute-start | bytes 786440 | tf_op jit(solution)/shard_map/ppermute | solution.py:24
  67.6 7.9 %copy-start.2 = (bf16[1,8,128,128]{3,2,1,0:T(8,128)(2,1)}, bf16[1,8,128,128]{3,2,1,0:T(8,128)(2,1)S(1)}, u32[]{:S(2)}) copy-start(bf16[1,8,128,128]{3,2,1,0:T(8,128)(2,1)S(1)} %collective-permute-done) | copy-start | bytes 786436
  67.7 7.2 %collective-permute-start.1 = (bf16[17,128,128]{2,1,0:T(8,128)(2,1)S(1)}, bf16[17,128,128]{2,1,0:T(8,128)(2,1)S(1)}, u32[]{:S(2)}, u32[]{:S(2)}) collective-permute-start(bf16[17,128,128]{2,1,0:T(8,128)(2,1)S(1)} %pad_maximum_fusion), channel_id=1, source_target_pairs={{0,15},{1,0},{2,1},{3,2},{4,3},{5,4},{6,5},{7,6},{8,7},{9,8},{10,9... | collective-permute-start | bytes 1671176 | tf_op jit(solution)/shard_map/ppermute | solution.py:24
  74.8 0.8 copy-start.1
  120.2 43.6 %copy-start.3 = (bf16[64,256]{1,0:T(8,128)(2,1)}, bf16[64,256]{1,0:T(8,128)(2,1)S(1)}, u32[]{:S(2)}) copy-start(bf16[64,256]{1,0:T(8,128)(2,1)S(1)} %reduce_sum.24) | copy-start | bytes 98308

commit v2 on v0

v2 whole, which is shorter than its diff:
```python
import jax
import jax.numpy as jnp
from jax import lax
from jax.experimental import pallas as pl
from jax.experimental.pallas import tpu as pltpu
from jax.sharding import PartitionSpec as P

VMEM = pl.BlockSpec(memory_space=pltpu.VMEM)
SMEM = pl.BlockSpec(memory_space=pltpu.SMEM)
NT = (((1,), (1,)), ((), ()))
BF16 = jnp.bfloat16
F32 = jnp.float32
MIB = 1 << 20


def dot(left, right):
    return jnp.dot(left, right, preferred_element_type=F32)


def dot_nt(left, right):
    return lax.dot_general(left, right, NT, preferred_element_type=F32)


def tree(terms):
    while len(terms) > 1:
        paired = [terms[k] + terms[k + 1] for k in range(0, len(terms) - 1, 2)]
        terms = paired + terms[len(terms) - len(terms) % 2 :]
    return terms[0]


def fold(value):
    half = value.shape[0] // 2
    return jnp.concatenate([value[:half], value[half:]], axis=1)


def unfold(value):
    half = value.shape[1] // 2
    return jnp.concatenate([value[:, :half], value[:, half:]], axis=0)


def shifted(value, axis, steps):
    count = lax.axis_size(axis)
    pairs = [(source, (source + steps) % count) for source in range(count)]
    return lax.ppermute(value, axis, pairs)


def rotate_kernel(x_ref, right_ref, out_ref):
    nb = right_ref.shape[2]
    for j in range(right_ref.shape[0]):
        x_now = x_ref[:, j * nb : (j + 1) * nb]
        for dq in range(2):
            out_ref[2 * j + dq] = dot_nt(x_now, right_ref[j, dq])


def prepare_kernel(index_ref, table_ref, cols_ref, u_ref, g_ref, splat_ref):
    n_pairs = u_ref.shape[0]
    fine_cols = n_pairs // 2
    nb = u_ref.shape[2]
    n_q = fine_cols // 2
    fine_rows = g_ref.shape[0] // 2

    def mix(i, carry):
        for dp in range(2):
            row = 2 * i + dp
            weights = []
            for pair in range(n_pairs):
                weight = table_ref[index_ref[(i * fine_cols + pair // 2) * 4 + 2 * dp + pair % 2]]
                weights.append(weight)
                splat_ref[row * n_pairs + pair] = jnp.full(splat_ref.shape[1:], weight, F32).astype(BF16)
            for q in range(n_q):
                total = None
                for dq in range(2):
                    if q < dq:
                        continue
                    first = 2 * (q - dq)
                    for j in range(first, min(first + 4, fine_cols)):
                        factor = jnp.where(cols_ref[j] + dq == q, weights[2 * j + dq], 0.0)
                        term = factor * u_ref[2 * j + dq]
                        total = term if total is None else total + term
                g_ref[row, :, q * nb : (q + 1) * nb] = total.astype(BF16)
        return carry

    lax.fori_loop(0, fine_rows, mix, 0)


CHUNKS = 8


def forward_kernel(rows_ref, foreign_ref, foreign_u_ref, left_ref, g_any, blocks_any, out_ref, tail_ref, g_ref, blocks_ref, t_ref, g_sem, b_sem):
    n_p, n_q, nb = blocks_ref.shape[:3]
    fine_rows = rows_ref.shape[0]
    n_dest = out_ref.shape[0]
    own = fine_rows // n_dest
    g_part = 2 * fine_rows // CHUNKS
    b_part = n_p // CHUNKS

    def g_copy(k):
        part = pl.ds(k * g_part, g_part)
        return pltpu.make_async_copy(g_any.at[part], g_ref.at[part], g_sem.at[k])

    def b_copy(k):
        part = pl.ds(k * b_part, b_part)
        return pltpu.make_async_copy(blocks_any.at[part], blocks_ref.at[part], b_sem.at[k])

    b_copy(0).start()
    for k in range(CHUNKS):
        g_copy(k).start()
        if k + 1 < CHUNKS:
            b_copy(k + 1).start()
    b_copy(0).wait()

    def whole(row):
        extra = foreign_ref[2 * row] * foreign_u_ref[0] + foreign_ref[2 * row + 1] * foreign_u_ref[1]
        first = (g_ref[row, :, :nb].astype(F32) + extra).astype(BF16)
        return jnp.concatenate([first, g_ref[row, :, nb:]], axis=1)

    def apply_some(k, carry):
        g_copy(k).wait()

        @pl.when(k + 1 < CHUNKS)
        def _():
            b_copy(k + 1).wait()

        for step in range(g_part // 2):
            i = k * (g_part // 2) + step
            for dp in range(2):
                p = jnp.minimum(rows_ref[i] + dp, n_p - 1)
                wide = jnp.concatenate([blocks_ref[p, q] for q in range(n_q)], axis=1)
                t_ref[i, :, dp * nb : (dp + 1) * nb] = dot_nt(whole(2 * i + dp), wide).astype(BF16)
        return carry

    lax.fori_loop(0, CHUNKS, apply_some, 0)
    for k in range(own):
        i = fine_rows - own + k
        t_ref[i, :, nb:] = jnp.zeros((t_ref.shape[1], nb), BF16)
        tail_ref[k] = whole(2 * i + 1)

    def finish_some(step, carry):
        for k in range(4):
            dest = 4 * step + k
            for half in range(own):
                i = dest * own + half
                y_now = dot(t_ref[i], left_ref[i].reshape(2 * nb, nb))
                out_ref[dest, :, half * nb : (half + 1) * nb] = y_now.astype(BF16)
        return carry

    lax.fori_loop(0, n_dest // 4, finish_some, 0)


def rim_kernel(main_ref, tail_ref, rim_row_ref, left_ref, rim_col_any, corner_any, out_ref):
    n_q, nb = rim_row_ref.shape[:2]
    last = out_ref.shape[0] - 1
    wide = jnp.concatenate([rim_row_ref[q] for q in range(n_q)], axis=1)
    for dest in range(last):
        out_ref[dest] = main_ref[dest]
    for k in range(left_ref.shape[0]):
        lanes = slice(k * nb, (k + 1) * nb)
        t_now = dot_nt(tail_ref[k], wide).astype(BF16)
        total = main_ref[last, :, lanes].astype(F32) + dot(t_now, left_ref[k])
        out_ref[last, :, lanes] = total.astype(BF16)


def adjoint_kernel(
    rows_ref,
    cols_ref,
    y_ref,
    rim_row_ref,
    rim_col_ref,
    corner_ref,
    left_ref,
    right_ref,
    splat_any,
    blocks_any,
    out_ref,
    s_ref,
    z_ref,
    splat_ref,
    blocks_ref,
    sems,
):
    n_p, n_q, nb = blocks_ref.shape[:3]
    fine_rows = left_ref.shape[0]
    fine_cols = right_ref.shape[0]
    n_dest = y_ref.shape[0]
    own = fine_rows // n_dest
    blocks_copy = pltpu.make_async_copy(blocks_any, blocks_ref, sems.at[0])
    splat_copy = pltpu.make_async_copy(splat_any, splat_ref, sems.at[1])
    blocks_copy.start()
    splat_copy.start()

    def rotate(step, carry):
        for k in range(4):
            dest = 4 * step + k
            for half in range(own):
                i = dest * own + half
                y_now = y_ref[dest, :, half * nb : (half + 1) * nb]
                for dp in range(2):
                    s_ref[2 * i + dp] = dot_nt(y_now, left_ref[i, dp]).astype(BF16)
        return carry

    lax.fori_loop(0, n_dest // 4, rotate, 0)
    blocks_copy.wait()

    def spread(row, block_of, rim):
        s_now = s_ref[row]
        for q in range(0, n_q, 2):
            moved = dot(s_now, jnp.concatenate([block_of(q), block_of(q + 1)], axis=1))
            z_ref[row, q] = fold(moved[:, :nb]).astype(BF16)
            z_ref[row, q + 1] = fold(moved[:, nb:]).astype(BF16)
        z_ref[row, n_q] = fold(dot(s_now, rim)).astype(BF16)

    def spread_row(i, dp):
        p = rows_ref[i] + dp
        spread(2 * i + dp, lambda q: blocks_ref[p, q], rim_col_ref[p])

    def spread_some(step, carry):
        for k in range(2):
            for dp in range(2):
                spread_row(2 * step + k, dp)
        return carry

    lax.fori_loop(0, fine_rows // 2 - 1, spread_some, 0)
    for i in (fine_rows - 2, fine_rows - 1):
        spread_row(i, 0)
        spread(2 * i + 1, lambda q: rim_row_ref[q], corner_ref[0])
    splat_copy.wait()

    def gather(j, carry):
        def add(group, sums):
            sums = list(sums)
            for dq in range(2):
                q = cols_ref[j] + dq
                terms = []
                for k in range(8):
                    row = 8 * group + k
                    factor = splat_ref[row * 2 * fine_cols + 2 * j + dq]
                    value = z_ref[row, q]
                    terms.append(value * jnp.concatenate([factor] * (value.shape[0] // 8), axis=0))
                sums[dq] = sums[dq] + tree(terms)
            return tuple(sums)

        start = jnp.zeros(z_ref.shape[2:], BF16)
        sums = lax.fori_loop(0, fine_rows // 4, add, (start, start))
        both = jnp.concatenate([unfold(part) for part in sums], axis=1)
        lanes = pl.ds(pl.multiple_of(j * nb, nb), nb)
        out_ref[:, lanes] = dot(both, right_ref[j].reshape(2 * nb, nb)).astype(BF16)
        return carry

    lax.fori_loop(0, fine_cols, gather, 0)


def exchange(value, axis):
    return lax.all_to_all(value, axis, split_axis=0, concat_axis=0, tiled=True)


def call(kernel, name, spaces, outs, scratch, limit, flops, args):
    specs = {"s": SMEM, "v": VMEM, "h": pl.BlockSpec(memory_space=pltpu.HBM), "a": pl.BlockSpec(memory_space=pl.ANY)}
    size = sum(a.size * a.dtype.itemsize for a in args)
    return pl.pallas_call(
        kernel,
        out_shape=[jax.ShapeDtypeStruct(shape, kind) for shape, kind in outs],
        in_specs=[specs[space] for space in spaces],
        out_specs=[VMEM] * len(outs),
        scratch_shapes=scratch,
        cost_estimate=pl.CostEstimate(flops=flops, bytes_accessed=size, transcendentals=0),
        compiler_params=pltpu.CompilerParams(vmem_limit_bytes=limit * MIB),
        name=name,
    )(*args)


def body(
    coarse_kernel,
    left_rotation,
    right_rotation,
    fine_map,
    coefficient_index,
    coefficient_table,
    trial_vectors,
):
    n_rows = lax.axis_size("rowk")
    n_cols = lax.axis_size("colk")
    row_id = lax.axis_index("rowk")
    col_id = lax.axis_index("colk")
    coarse_total = coarse_kernel.shape[1]
    fine_rows = left_rotation.shape[0]
    fine_cols = right_rotation.shape[0]
    nb = left_rotation.shape[2]
    vecs = trial_vectors.shape[0]
    coarse_rows = coarse_total // n_rows
    coarse_cols = coarse_total // n_cols
    own = fine_rows // n_cols
    n_pairs = 2 * fine_cols
    dma = pltpu.SemaphoreType.DMA

    blocks = exchange(coarse_kernel.reshape(n_cols, coarse_cols, nb, nb), "colk")

    rows = lax.dynamic_slice_in_dim(fine_map, row_id * fine_rows, fine_rows) - row_id * coarse_rows
    cols = lax.dynamic_slice_in_dim(fine_map, col_id * fine_cols, fine_cols) - col_id * coarse_cols
    entries = jnp.arange(coefficient_table.shape[0], dtype=jnp.int32)
    table = jnp.where(entries > 0, coefficient_table, jnp.zeros_like(coefficient_table))
    edge = coefficient_index[:, fine_cols - 2 :, 1::2].transpose(0, 2, 1).reshape(-1)
    edge = jnp.sum(jnp.where(edge[:, None] == entries, table, jnp.zeros_like(table)), axis=-1)
    (u,) = call(rotate_kernel, "rotate", "vv", [((n_pairs, vecs, nb), F32)], [], 4, 10**8, (trial_vectors, right_rotation))
    foreign = shifted(edge, "colk", 1)
    foreign_u = shifted(jnp.stack([u[n_pairs - 3], u[n_pairs - 1]]), "colk", 1)
    g, splat = call(
        prepare_kernel,
        "prepare",
        "sssv",
        [((2 * fine_rows, vecs, coarse_cols * nb), BF16), ((2 * fine_rows * n_pairs, 8, 2 * nb), BF16)],
        [],
        24,
        10**9,
        (coefficient_index.reshape(-1), table, cols, u),
    )
    blocks, g, splat, rows, cols = lax.optimization_barrier((blocks, g, splat, rows, cols))

    rim_row = shifted(blocks[0], "rowk", -1)
    rim_col = shifted(blocks[:, 0], "colk", -1)
    pairs = []
    for r in range(n_rows):
        for c in range(n_cols):
            pairs.append((((r + 1) % n_rows) * n_cols + (c + 1) % n_cols, r * n_cols + c))
    corner = lax.ppermute(blocks[0, 0:1], ("rowk", "colk"), pairs)

    block_buffer = pltpu.VMEM((coarse_rows, coarse_cols, nb, nb), BF16)
    main, tail = call(
        forward_kernel,
        "forward",
        "ssvvhh",
        [((n_cols, vecs, own * nb), BF16), ((own, vecs, coarse_cols * nb), BF16)],
        [
            pltpu.VMEM((2 * fine_rows, vecs, coarse_cols * nb), BF16),
            block_buffer,
            pltpu.VMEM((fine_rows, vecs, 2 * nb), BF16),
            dma((CHUNKS,)),
            dma((CHUNKS,)),
        ],
        52,
        10**9,
        (rows, foreign, foreign_u, left_rotation, g, blocks),
    )
    (partial,) = call(
        rim_kernel,
        "rim",
        "vvvvaa",
        [((n_cols, vecs, own * nb), BF16)],
        [],
        8,
        10**8,
        (main, tail, rim_row, left_rotation[fine_rows - own :, 1], rim_col, corner),
    )

    forward_image = jnp.sum(exchange(partial, "colk").astype(F32), axis=0).astype(BF16)
    copies = lax.optimization_barrier(jnp.broadcast_to(forward_image, (n_cols, vecs, own * nb)))
    row_image = exchange(copies, "colk")

    (terms,) = call(
        adjoint_kernel,
        "adjoint",
        "ssvvvvvvhh",
        [((vecs, fine_cols * nb), BF16)],
        [
            pltpu.VMEM((2 * fine_rows, vecs, nb), BF16),
            pltpu.VMEM((2 * fine_rows, coarse_cols + 1, vecs // 2, 2 * nb), BF16),
            pltpu.VMEM((2 * fine_rows * n_pairs, 8, 2 * nb), BF16),
            block_buffer,
            dma((2,)),
        ],
        52,
        10**9,
        (rows, cols, row_image, rim_row, rim_col, corner, left_rotation, right_rotation, splat, blocks),
    )

    terms = terms.reshape(n_rows, vecs // n_rows, fine_cols * nb)
    adjoint_image = jnp.sum(exchange(terms, "rowk").astype(F32), axis=0).astype(BF16)
    return (forward_image, adjoint_image)


def solution(mesh):
    return jax.shard_map(
        body,
        mesh=mesh,
        in_specs=(
            P(("rowk", "colk"), None, None, None),
            P("rowk", None, None, None),
            P("colk", None, None, None),
            P(),
            P("rowk", "colk", None),
            P(),
            P(None, "colk"),
        ),
        out_specs=(P(None, ("rowk", "colk")), P("rowk", "colk")),
        check_vma=False,
    )
```

time: 507 us -> 143 us (0.28)
  matrix products: 152 us -> 0 us
  waiting for transfers between devices: 147 us -> 34.1 us
  local copies, waits for them, and re-layouts: 104 us -> 10.8 us
  Pallas kernels: 0 us -> 38.5 us
  blocking collectives: 73.8 us -> 42.6 us
  between operations: 14.1 us -> 0.87 us
  starting transfers between devices: 6.65 us -> 14.3 us
  other arithmetic: 7.89 us -> 0.98 us
    dot_general x18 -> x0, matrix products: 152 us -> none  [the longest x8 71.8 us: build_rows(): jnp.einsum('ipjqab,jqbc->ipjqac', picked, right_rotation, preferred_eleme...]
    reduce_scatter x2 -> x0, waiting for transfers between devices: 136 us -> none  [the longest x1 70.8 us: body(): lax.psum_scatter(terms.reshape(vec_count // n_rows * lax.axis_size('rowk'...]
    gather x8 -> x0, local copies, waits for them, and re-layouts: 97.4 us -> none  [build_rows(): local_blocks[sources[:, :, None, None], col_source[None, None, :, :]]]
    pallas_call x0 -> x5, Pallas kernels: none -> 38.5 us  [call(): pl.pallas_call(kernel, out_shape=[jax.ShapeDtypeStruct(shape, kind) for s...]
    all_to_all x0 -> x1, waiting for transfers between devices: none -> 34.1 us  [exchange(): return lax.all_to_all(value, axis, split_axis=0, concat_axis=0, tiled=True)]
    all_gather x1 -> x0, blocking collectives: 17.9 us -> none  [body(): row_image = lax.all_gather(forward_image, 'colk', axis=1, tiled=True)]
    all_to_all x1 -> x3, blocking collectives: 55.8 us -> 42.6 us  [exchange(): return lax.all_to_all(value, axis, split_axis=0, concat_axis=0, tiled=True)]
    ppermute x2 -> x4, waiting for transfers between devices: 11.3 us -> 0.01 us  [shifted(): return lax.ppermute(value, axis, pairs)]
  transfers between devices with their start and end apart: 4 -> 6, of which waited for: 4 -> 1; matrix products, arithmetic and copies ran while one was open for 0% -> 3% of each run, Pallas kernels for 0% -> 16%
where the time goes in v2:
time: 143 us; the launch traced here: 142 us
  blocking collectives  42.6 us (30%)
  Pallas kernels  38.5 us (27%)
  waiting for transfers between devices  34.1 us (24%)
  starting transfers between devices  14.3 us (10%)
  local copies, waits for them, and re-layouts  10.8 us (8%)
    all_to_all x3, blocking collectives, exchange(): return lax.all_to_all(value, axis, split_axis=0, concat_axis=0, tiled=True)  42.6 us
    pallas_call x5, Pallas kernels, call(): pl.pallas_call(kernel, out_shape=[jax.ShapeDtypeStruct(shape, kind) for s...  38.5 us
    all_to_all x1, waiting for transfers between devices, exchange(): return lax.all_to_all(value, axis, split_axis=0, concat_axis=0, tiled=True)  34.1 us
    ppermute x4, starting transfers between devices, shifted(): return lax.ppermute(value, axis, pairs)  8.59 us
    unnamed x17, local copies, waits for them, and re-layouts  6.68 us
    all_to_all x1, starting transfers between devices, exchange(): return lax.all_to_all(value, axis, split_axis=0, concat_axis=0, tiled=True)  5.72 us
  transfers between devices with their start and end apart: 6, of which 1 were waited for; matrix products, arithmetic and copies ran while one was open for 3% of the time, Pallas kernels for 16%

profile of v2, /device:TPU:0, one launch (start us, length us, event | category | flops | bytes accessed | tf_op | source)
XLA Modules:
  0.0 142.2 jit_solution(12066392617167747663)
XLA Ops:
  0.6 0.0 copy-start.2
  0.6 0.0 copy-start.3
  0.7 0.0 copy-start.5
  0.7 0.0 copy-start.7
  0.7 0.0 copy-start.6
  0.7 5.7 %all-to-all-start = ((bf16[16,8,128,128]{3,2,1,0:T(8,128)(2,1)}), bf16[16,8,128,128]{3,2,1,0:T(8,128)(2,1)}, u32[]{:S(2)}, u32[]{:S(2)}) async-start(bf16[16,8,128,128]{3,2,1,0:T(8,128)(2,1)} %bitcast.14), calls=%async_computation | async-start | bytes 8388608 | tf_op jit(solution)/shard_map/all_to_all | solution.py:253
  6.4 0.0 copy-done.2
  6.4 0.0 copy-done.3
  6.4 0.8 rotate.1.u_ref
  7.3 0.4 collective-permute-start.1
  7.7 0.0 copy-done.5
  7.7 0.1 copy.15
  7.8 0.1 eq.15
  8.0 0.0 copy-done.7
  8.0 0.1 select_reduce_fusion
  8.1 1.6 %collective-permute-start = (f32[128]{0:T(128)S(1)}, f32[128]{0:T(128)S(1)}, u32[]{:S(2)}, u32[]{:S(2)}) collective-permute-start(f32[128]{0:T(128)S(1)} %select_reduce_fusion), channel_id=1, source_target_pairs={{0,1},{1,2},{2,3},{3,4},{4,5},{5,6},{6,7},{7,8},{8,9},{9,10},{10,1... | collective-permute-start | bytes 1544 | tf_op jit(solution)/shard_map/ppermute | solution.py:44
  9.7 0.2 copy.14
  10.0 0.2 reshape.15.index_ref
  10.1 0.0 copy-done.6
  10.1 0.1 dynamic-slice_subtract_fusion.1.cols_ref
  10.2 11.2 %prepare.1 = (bf16[64,64,1024]{2,1,0:T(8,128)(2,1)S(1)}, bf16[2048,8,256]{2,1,0:T(8,128)(2,1)S(1)}) custom-call(s32[2048]{0:T(1024)S(1)} %reshape.15.index_ref, f32[16]{0:T(128)S(1)} %compare_select_fusion.table_ref, s32[16]{0:T(128)S(1)} %dynamic-slice_subtract_fusion.1.cols_ref, f32[32,64,128]{2,1,0:T(8,128)S(1)} %rotate.1.u_ref), custom_call_target="tpu_custom_call" | custom-call | flops 1000000000 | bytes 1056896 | tf_op jit(solution)/shard_map/prepare/pallas_call | solution.py:259
  21.4 0.0 copy-start
  21.4 3.2 %copy-done = bf16[2048,8,256]{2,1,0:T(8,128)(2,1)} copy-done((bf16[2048,8,256]{2,1,0:T(8,128)(2,1)}, bf16[2048,8,256]{2,1,0:T(8,128)(2,1)S(1)}, u32[]{:S(2)}) %copy-start) | copy-done | bytes 8388632
  24.7 3.2 %copy-done.1 = bf16[64,64,1024]{2,1,0:T(8,128)(2,1)} copy-done((bf16[64,64,1024]{2,1,0:T(8,128)(2,1)}, bf16[64,64,1024]{2,1,0:T(8,128)(2,1)S(1)}, u32[]{:S(2)}) %copy-start.1) | copy-done | bytes 8388632
  27.9 0.1 dynamic-slice_subtract_fusion.rows_ref
  28.0 0.8 slice_bitcast_fusion.2.left_ref
  28.8 34.1 %all-to-all-done.blocks_any = bf16[16,8,128,128]{3,2,1,0:T(8,128)(2,1)} async-done(((bf16[16,8,128,128]{3,2,1,0:T(8,128)(2,1)}), bf16[16,8,128,128]{3,2,1,0:T(8,128)(2,1)}, u32[]{:S(2)}, u32[]{:S(2)}) %all-to-all-start) | async-done | bytes 4194336 | tf_op jit(solution)/shard_map/all_to_all | solution.py:253
  62.9 1.1 slice_bitcast_fusion
  64.0 0.1 collective-permute-start.3
  64.0 1.0 slice_bitcast_fusion.1
  65.0 6.4 %collective-permute-start.2 = (bf16[8,128,128]{2,1,0:T(8,128)(2,1)S(1)}, bf16[8,128,128]{2,1,0:T(8,128)(2,1)S(1)}, u32[]{:S(2)}, u32[]{:S(2)}) collective-permute-start(bf16[8,128,128]{2,1,0:T(8,128)(2,1)S(1)} %slice_bitcast_fusion.1), channel_id=1, source_target_pairs={{0,112},{16,0},{32,16},{48,32},{64,48},{80,64},{96,80},{112,96},{1... | collective-permute-start | bytes 786440 | tf_op jit(solution)/shard_map/ppermute | solution.py:44
  71.5 0.8 slice_bitcast_fusion.3
  72.2 0.0 collective-permute-start.4
  72.2 0.0 collective-permute-done.foreign_ref
  72.2 0.0 collective-permute-done.1.foreign_u_ref
  72.2 10.9 %forward.1 = (bf16[16,64,256]{2,1,0:T(8,128)(2,1)S(1)}, bf16[2,64,1024]{2,1,0:T(8,128)(2,1)S(1)}) custom-call(s32[32]{0:T(128)S(1)} %dynamic-slice_subtract_fusion.rows_ref, f32[128]{0:T(128)S(1)} %collective-permute-done.foreign_ref, f32[2,64,128]{2,1,0:T(8,128)S(1)} %collective-permute-done.1.foreign_u_ref, bf16[32,2,128,128]{3,2,1,0:T(8,128)(2,1)} %left_ref.3, ...), custom_call_target="tpu_custom_call" | custom-call | flops 1000000000 | bytes 14746240 | tf_op jit(solution)/shard_map/forward/pallas_call | solution.py:259
  83.1 0.0 collective-permute-done.4.corner_any.corner_ref
  83.1 0.0 collective-permute-done.2.rim_row_ref
  83.2 0.0 collective-permute-done.3.rim_col_any.rim_col_ref
  83.2 0.6 rim.1
  83.8 16.5 %all_to_all.20 = bf16[16,64,256]{2,1,0:T(8,128)(2,1)S(1)} all-to-all(bf16[16,64,256]{2,1,0:T(8,128)(2,1)S(1)} %rim.1), channel_id=1, replica_groups=mesh['rowk'=8,'colk'=16] {'colk'}, dimensions={0} | all-to-all | bytes 1048576 | tf_op jit(solution)/shard_map/all_to_all | solution.py:253
  100.3 0.1 reduce_sum.34
  100.4 0.0 copy-start.4
  100.4 13.5 %all_to_all.21.y_ref = bf16[16,64,256]{2,1,0:T(8,128)(2,1)S(1)} all-to-all(bf16[16,64,256]{2,1,0:T(8,128)(2,1)S(1)} %broadcast_in_dim.14), channel_id=1, replica_groups=mesh['rowk'=8,'colk'=16] {'colk'}, dimensions={0} | all-to-all | bytes 1048576 | tf_op jit(solution)/shard_map/all_to_all | solution.py:253
  113.9 14.9 %adjoint.1 = bf16[64,2048]{1,0:T(8,128)(2,1)S(1)} custom-call(s32[32]{0:T(128)S(1)} %dynamic-slice_subtract_fusion.rows_ref, s32[16]{0:T(128)S(1)} %dynamic-slice_subtract_fusion.1.cols_ref, bf16[16,64,256]{2,1,0:T(8,128)(2,1)S(1)} %all_to_all.21.y_ref, bf16[8,128,128]{2,1,0:T(8,128)(2,1)S(1)} %collective-permute-done.2.rim_row_ref, ...), custom_call_target="tpu_custom_call" | custom-call | flops 1000000000 | bytes 17072320 | tf_op jit(solution)/shard_map/adjoint/pallas_call | solution.py:259
  128.8 0.0 copy-done.4
  128.8 12.7 %all_to_all.22 = bf16[8,8,2048]{2,1,0:T(8,128)(2,1)S(1)} all-to-all(bf16[8,8,2048]{2,1,0:T(8,128)(2,1)S(1)} %bitcast.13), channel_id=1, replica_groups=mesh['rowk'=8,'colk'=16] {'rowk'}, dimensions={0} | all-to-all | bytes 524288 | tf_op jit(solution)/shard_map/all_to_all | solution.py:253
  141.5 0.7 reduce_sum.35
  (6 shorter events, 0.1 us)
Async XLA Ops:
  0.6 5.8 %copy-start.2 = (bf16[16,2,128,128]{3,2,1,0:T(8,128)(2,1)S(1)}, bf16[16,2,128,128]{3,2,1,0:T(8,128)(2,1)}, u32[]{:S(2)}) copy-start(bf16[16,2,128,128]{3,2,1,0:T(8,128)(2,1)} %right_ref.3) | copy-start | bytes 3145732
  0.6 5.8 %copy-start.3 = (bf16[64,2048]{1,0:T(8,128)(2,1)S(1)}, bf16[64,2048]{1,0:T(8,128)(2,1)}, u32[]{:S(2)}) copy-start(bf16[64,2048]{1,0:T(8,128)(2,1)} %x_ref.1) | copy-start | bytes 786436
  0.7 7.1 %copy-start.5 = (s32[32,16,4]{0,2,1:T(4,128)S(1)}, s32[32,16,4]{0,2,1:T(4,128)}, u32[]{:S(2)}) copy-start(s32[32,16,4]{0,2,1:T(4,128)} %param.11) | copy-start | bytes 24580
  0.7 7.3 %copy-start.7 = (f32[16]{0:T(128)S(1)}, f32[16]{0:T(128)}, u32[]{:S(2)}) copy-start(f32[16]{0:T(128)} %param.12) | copy-start | bytes 196
  0.7 9.5 %copy-start.6 = (s32[256]{0:T(256)S(1)}, s32[256]{0:T(256)}, u32[]{:S(2)}) copy-start(s32[256]{0:T(256)} %param.10) | copy-start | bytes 3076
  0.7 62.2 %all-to-all-start = ((bf16[16,8,128,128]{3,2,1,0:T(8,128)(2,1)}), bf16[16,8,128,128]{3,2,1,0:T(8,128)(2,1)}, u32[]{:S(2)}, u32[]{:S(2)}) async-start(bf16[16,8,128,128]{3,2,1,0:T(8,128)(2,1)} %bitcast.14), calls=%async_computation | async-start | bytes 8388608 | tf_op jit(solution)/shard_map/all_to_all | solution.py:253
  7.3 64.9 %collective-permute-start.1 = (f32[2,64,128]{2,1,0:T(8,128)S(1)}, f32[2,64,128]{2,1,0:T(8,128)S(1)}, u32[]{:S(2)}, u32[]{:S(2)}) collective-permute-start(f32[2,64,128]{2,1,0:T(8,128)S(1)} %pad_maximum_fusion), channel_id=1, source_target_pairs={{0,1},{1,2},{2,3},{3,4},{4,5},{5,6},{6,7},{7,8},{8,9},{9,10},{10,1... | collective-permute-start | bytes 196616 | tf_op jit(solution)/shard_map/ppermute | solution.py:44
  8.1 64.1 %collective-permute-start = (f32[128]{0:T(128)S(1)}, f32[128]{0:T(128)S(1)}, u32[]{:S(2)}, u32[]{:S(2)}) collective-permute-start(f32[128]{0:T(128)S(1)} %select_reduce_fusion), channel_id=1, source_target_pairs={{0,1},{1,2},{2,3},{3,4},{4,5},{5,6},{6,7},{7,8},{8,9},{9,10},{10,1... | collective-permute-start | bytes 1544 | tf_op jit(solution)/shard_map/ppermute | solution.py:44
  21.4 3.2 %copy-start = (bf16[2048,8,256]{2,1,0:T(8,128)(2,1)}, bf16[2048,8,256]{2,1,0:T(8,128)(2,1)S(1)}, u32[]{:S(2)}) copy-start(bf16[2048,8,256]{2,1,0:T(8,128)(2,1)S(1)} %get-tuple-element.19.splat_any) | copy-start | bytes 25165828
  24.6 3.2 %copy-start.1 = (bf16[64,64,1024]{2,1,0:T(8,128)(2,1)}, bf16[64,64,1024]{2,1,0:T(8,128)(2,1)S(1)}, u32[]{:S(2)}) copy-start(bf16[64,64,1024]{2,1,0:T(8,128)(2,1)S(1)} %get-tuple-element.14.g_any) | copy-start | bytes 25165828
  64.0 19.2 %collective-permute-start.3 = (bf16[16,128,128]{2,1,0:T(8,128)(2,1)S(1)}, bf16[16,128,128]{2,1,0:T(8,128)(2,1)S(1)}, u32[]{:S(2)}, u32[]{:S(2)}) collective-permute-start(bf16[16,128,128]{2,1,0:T(8,128)(2,1)S(1)} %slice_bitcast_fusion), channel_id=1, source_target_pairs={{0,15},{1,0},{2,1},{3,2},{4,3},{5,4},{6,5},{7,6},{8,7},{9,8},{10,9... | collective-permute-start | bytes 1572872 | tf_op jit(solution)/shard_map/ppermute | solution.py:44
  65.0 18.1 %collective-permute-start.2 = (bf16[8,128,128]{2,1,0:T(8,128)(2,1)S(1)}, bf16[8,128,128]{2,1,0:T(8,128)(2,1)S(1)}, u32[]{:S(2)}, u32[]{:S(2)}) collective-permute-start(bf16[8,128,128]{2,1,0:T(8,128)(2,1)S(1)} %slice_bitcast_fusion.1), channel_id=1, source_target_pairs={{0,112},{16,0},{32,16},{48,32},{64,48},{80,64},{96,80},{112,96},{1... | collective-permute-start | bytes 786440 | tf_op jit(solution)/shard_map/ppermute | solution.py:44
  72.2 10.9 %collective-permute-start.4 = (bf16[1,128,128]{2,1,0:T(8,128)(2,1)S(1)}, bf16[1,128,128]{2,1,0:T(8,128)(2,1)S(1)}, u32[]{:S(2)}, u32[]{:S(2)}) collective-permute-start(bf16[1,128,128]{2,1,0:T(8,128)(2,1)S(1)} %slice_bitcast_fusion.3), channel_id=1, source_target_pairs={{17,0},{18,1},{19,2},{20,3},{21,4},{22,5},{23,6},{24,7},{25,8},{26... | collective-permute-start | bytes 98312 | tf_op jit(solution)/shard_map/ppermute | solution.py:324
  100.4 28.4 %copy-start.4 = (bf16[64,256]{1,0:T(8,128)(2,1)}, bf16[64,256]{1,0:T(8,128)(2,1)S(1)}, u32[]{:S(2)}) copy-start(bf16[64,256]{1,0:T(8,128)(2,1)S(1)} %reduce_sum.34) | copy-start | bytes 98308

commit v3 on v2

v3 whole, which is shorter than its diff:
```python
import jax
import jax.numpy as jnp
from jax import lax
from jax.experimental import pallas as pl
from jax.experimental.pallas import tpu as pltpu
from jax.sharding import PartitionSpec as P

VMEM = pl.BlockSpec(memory_space=pltpu.VMEM)
SMEM = pl.BlockSpec(memory_space=pltpu.SMEM)
NT = (((1,), (1,)), ((), ()))
BF16 = jnp.bfloat16
F32 = jnp.float32
MIB = 1 << 20


def dot(left, right):
    return jnp.dot(left, right, preferred_element_type=F32)


def dot_nt(left, right):
    return lax.dot_general(left, right, NT, preferred_element_type=F32)


def tree(terms):
    while len(terms) > 1:
        paired = [terms[k] + terms[k + 1] for k in range(0, len(terms) - 1, 2)]
        terms = paired + terms[len(terms) - len(terms) % 2 :]
    return terms[0]


def fold(value):
    half = value.shape[0] // 2
    return jnp.concatenate([value[:half], value[half:]], axis=1)


def unfold(value):
    half = value.shape[1] // 2
    return jnp.concatenate([value[:, :half], value[:, half:]], axis=0)


def shifted(value, axis, steps):
    count = lax.axis_size(axis)
    pairs = [(source, (source + steps) % count) for source in range(count)]
    return lax.ppermute(value, axis, pairs)


def rotate_kernel(x_ref, right_ref, out_ref):
    nb = right_ref.shape[2]
    for j in range(right_ref.shape[0]):
        x_now = x_ref[:, j * nb : (j + 1) * nb]
        for dq in range(2):
            out_ref[2 * j + dq] = dot_nt(x_now, right_ref[j, dq])


def prepare_kernel(index_ref, table_ref, cols_ref, order_ref, u_ref, g_ref, splat_ref):
    n_pairs = u_ref.shape[0]
    fine_cols = n_pairs // 2
    nb = u_ref.shape[2]
    n_q = fine_cols // 2
    def mix(place, carry):
        row = order_ref[place]
        base = (row // 2) * fine_cols * 4 + 2 * (row % 2)
        weights = []
        for pair in range(n_pairs):
            weight = table_ref[index_ref[base + (pair // 2) * 4 + pair % 2]]
            weights.append(weight)
            splat_ref[pair * g_ref.shape[0] + row] = jnp.full(splat_ref.shape[1:], weight, F32).astype(BF16)
        for q in range(n_q):
            total = None
            for dq in range(2):
                if q < dq:
                    continue
                first = 2 * (q - dq)
                for j in range(first, min(first + 4, fine_cols)):
                    factor = jnp.where(cols_ref[j] + dq == q, weights[2 * j + dq], 0.0)
                    term = factor * u_ref[2 * j + dq]
                    total = term if total is None else total + term
            g_ref[place, :, q * nb : (q + 1) * nb] = total.astype(BF16)
        return carry

    lax.fori_loop(0, g_ref.shape[0], mix, 0)


CHUNKS = 8


def forward_kernel(
    order_ref,
    place_ref,
    start_ref,
    foreign_ref,
    foreign_u_ref,
    left_any,
    g_any,
    blocks_any,
    out_ref,
    tail_ref,
    g_ref,
    blocks_ref,
    t_ref,
    left_ref,
    g_sem,
    b_sem,
    left_sem,
):
    n_p, n_q, nb = blocks_ref.shape[:3]
    n_rows = order_ref.shape[0]
    vecs = g_ref.shape[1]
    n_dest = out_ref.shape[0]
    own = n_rows // 2 // n_dest
    g_part = n_rows // CHUNKS
    b_part = n_p // CHUNKS

    def g_copy(k):
        part = pl.ds(k * g_part, g_part)
        return pltpu.make_async_copy(g_any.at[part], g_ref.at[part], g_sem.at[k])

    def b_copy(k):
        part = pl.ds(k * b_part, b_part)
        return pltpu.make_async_copy(blocks_any.at[part], blocks_ref.at[part], b_sem.at[k])

    for k in range(CHUNKS):
        b_copy(k).start()
        g_copy(k).start()
    left_copy = pltpu.make_async_copy(left_any, left_ref, left_sem.at[0])
    left_copy.start()

    def whole(at):
        row = order_ref[jnp.minimum(at, n_rows - 1)]
        extra = foreign_ref[2 * row] * foreign_u_ref[0] + foreign_ref[2 * row + 1] * foreign_u_ref[1]
        first = (g_ref[at, :, :nb].astype(F32) + extra).astype(BF16)
        return jnp.concatenate([first, g_ref[at, :, nb:]], axis=1)

    def apply(p):
        wide = jnp.concatenate([blocks_ref[p, q] for q in range(n_q)], axis=1)
        first = start_ref[p]

        def some(at, count):
            lines = jnp.concatenate([whole(at + k) for k in range(count)], axis=0)
            moved = dot_nt(lines, wide).astype(BF16)
            for k in range(count):
                t_ref[at + k] = moved[k * vecs : (k + 1) * vecs]

        some(first, 4)

        @pl.when(start_ref[p + 1] > first + 4)
        def _():
            some(first + 4, 2)

    def step(k, carry):
        b_copy(k).wait()

        @pl.when(k == 0)
        def _():
            g_copy(k).wait()

        @pl.when(k + 1 < CHUNKS)
        def _():
            g_copy(k + 1).wait()

        apply(2 * k)
        apply(2 * k + 1)
        return carry

    lax.fori_loop(0, CHUNKS, step, 0)
    for k in range(own):
        tail_ref[k] = whole(n_rows - own + k)
        t_ref[n_rows - own + k] = jnp.zeros(t_ref.shape[1:], BF16)
    left_copy.wait()

    def finish_some(step, carry):
        for k in range(4):
            dest = 4 * step + k
            for half in range(own):
                i = dest * own + half
                both = jnp.concatenate([t_ref[place_ref[2 * i]], t_ref[place_ref[2 * i + 1]]], axis=1)
                y_now = dot(both, left_ref[i].reshape(2 * nb, nb))
                out_ref[dest, :, half * nb : (half + 1) * nb] = y_now.astype(BF16)
        return carry

    lax.fori_loop(0, n_dest // 4, finish_some, 0)


def rim_kernel(main_ref, tail_ref, rim_row_ref, left_ref, col_any, out_ref):
    n_q, nb = rim_row_ref.shape[:2]
    last = out_ref.shape[0] - 1
    wide = jnp.concatenate([rim_row_ref[q] for q in range(n_q)], axis=1)
    for dest in range(last):
        out_ref[dest] = main_ref[dest]
    for k in range(left_ref.shape[0]):
        lanes = slice(k * nb, (k + 1) * nb)
        t_now = dot_nt(tail_ref[k], wide).astype(BF16)
        total = main_ref[last, :, lanes].astype(F32) + dot(t_now, left_ref[k])
        out_ref[last, :, lanes] = total.astype(BF16)


def adjoint_kernel(
    rows_ref,
    cols_ref,
    y_ref,
    rim_row_ref,
    rim_col_ref,
    corner_ref,
    left_ref,
    right_ref,
    splat_any,
    blocks_any,
    out_ref,
    s_ref,
    z_ref,
    splat_ref,
    blocks_ref,
    col_ref,
    sems,
):
    n_p, n_q, nb = blocks_any.shape[:3]
    fine_rows = left_ref.shape[0]
    fine_cols = right_ref.shape[0]
    n_dest = y_ref.shape[0]
    own = fine_rows // n_dest
    group = 8
    stages = list(range(0, n_q + 1, 2)) + [None]
    ends = [fine_cols if q is None else max(2 * q - 2, 0) for q in stages]
    waits = []
    for number, q in enumerate(stages):
        copies = []
        if q is not None and q < n_q:
            columns = pl.ds(q, 2)
            copies.append((blocks_any.at[:, columns], blocks_ref.at[pl.ds(0, n_p), columns]))
        begin = ends[number - 1] if number > 0 else 0
        if ends[number] > begin:
            lines = pl.ds(begin * 4 * fine_rows, (ends[number] - begin) * 4 * fine_rows)
            copies.append((splat_any.at[lines], splat_ref.at[lines]))
        started = []
        for kind, (source, target) in enumerate(copies):
            started.append(pltpu.make_async_copy(source, target, sems.at[2 * number + kind]))
            started[-1].start()
        waits.append(started)

    def rotate(step, carry):
        for k in range(4):
            dest = 4 * step + k
            for half in range(own):
                i = dest * own + half
                y_now = y_ref[dest, :, half * nb : (half + 1) * nb]
                moved = dot_nt(y_now, left_ref[i].reshape(2 * nb, nb)).astype(BF16)
                s_ref[2 * i] = moved[:, :nb]
                s_ref[2 * i + 1] = moved[:, nb:]
        return carry

    lax.fori_loop(0, n_dest // 4, rotate, 0)
    for q in range(n_q):
        blocks_ref[n_p, q] = rim_row_ref[q]
    for p in range(n_p):
        col_ref[p] = rim_col_ref[p]
    col_ref[n_p] = corner_ref[0]

    def spread(row, p, q):
        if q < n_q:
            moved = dot(s_ref[row], jnp.concatenate([blocks_ref[p, q], blocks_ref[p, q + 1]], axis=1))
            return [(q, fold(moved[:, :nb]).astype(BF16)), (q + 1, fold(moved[:, nb:]).astype(BF16))]
        return [(q, fold(dot(s_ref[row], col_ref[p])).astype(BF16))]

    def stage(columns, q):
        def body(part, sums):
            sums = list(sums)
            for number, (j, dq) in enumerate(columns):
                source = cols_ref[j] + dq
                terms = []
                for k in range(group):
                    row = group * part + k
                    factor = splat_ref[(2 * j + dq) * 2 * fine_rows + row]
                    value = z_ref[row, source]
                    terms.append(value * jnp.concatenate([factor] * (value.shape[0] // 8), axis=0))
                sums[number] = sums[number] + tree(terms)
            if q is not None:
                results = []
                for k in range(group):
                    row = group * part + k
                    p = rows_ref[group // 2 * part + k // 2] + k % 2
                    results.append((row, spread(row, p, q)))
                for row, pieces in results:
                    for at, piece in pieces:
                        z_ref[row, at] = piece
            return tuple(sums)

        start = tuple(jnp.zeros(z_ref.shape[2:], BF16) for _ in columns)
        sums = lax.fori_loop(0, 2 * fine_rows // group, body, start)
        for number in range(0, len(columns), 2):
            j = columns[number][0]
            both = jnp.concatenate([unfold(part) for part in sums[number : number + 2]], axis=1)
            out_ref[:, j * nb : (j + 1) * nb] = dot(both, right_ref[j].reshape(2 * nb, nb)).astype(BF16)

    done = 0
    for number, q in enumerate(stages):
        ready = ends[number]
        for copy in waits[number]:
            copy.wait()
        stage([(j, dq) for j in range(done, ready) for dq in range(2)], q)
        done = ready


def share_kernel(parts_ref, image_ref, copies_ref):
    total = parts_ref[0].astype(F32)
    for k in range(1, parts_ref.shape[0]):
        total = total + parts_ref[k].astype(F32)
    image = total.astype(BF16)
    image_ref[...] = image
    for k in range(copies_ref.shape[0]):
        copies_ref[k] = image


def exchange(value, axis):
    return lax.all_to_all(value, axis, split_axis=0, concat_axis=0, tiled=True)


def call(kernel, name, spaces, outs, scratch, limit, flops, args):
    specs = {"s": SMEM, "v": VMEM, "h": pl.BlockSpec(memory_space=pltpu.HBM), "a": pl.BlockSpec(memory_space=pl.ANY)}
    size = sum(a.size * a.dtype.itemsize for a in args)
    return pl.pallas_call(
        kernel,
        out_shape=[jax.ShapeDtypeStruct(shape, kind) for shape, kind in outs],
        in_specs=[specs[space] for space in spaces],
        out_specs=[VMEM] * len(outs),
        scratch_shapes=scratch,
        cost_estimate=pl.CostEstimate(flops=flops, bytes_accessed=size, transcendentals=0),
        compiler_params=pltpu.CompilerParams(vmem_limit_bytes=limit * MIB),
        name=name,
    )(*args)


def body(
    coarse_kernel,
    left_rotation,
    right_rotation,
    fine_map,
    coefficient_index,
    coefficient_table,
    trial_vectors,
):
    n_rows = lax.axis_size("rowk")
    n_cols = lax.axis_size("colk")
    row_id = lax.axis_index("rowk")
    col_id = lax.axis_index("colk")
    coarse_total = coarse_kernel.shape[1]
    fine_rows = left_rotation.shape[0]
    fine_cols = right_rotation.shape[0]
    nb = left_rotation.shape[2]
    vecs = trial_vectors.shape[0]
    coarse_rows = coarse_total // n_rows
    coarse_cols = coarse_total // n_cols
    own = fine_rows // n_cols
    n_pairs = 2 * fine_cols
    dma = pltpu.SemaphoreType.DMA

    blocks = exchange(coarse_kernel.reshape(n_cols, coarse_cols, nb, nb), "colk")

    rows = lax.dynamic_slice_in_dim(fine_map, row_id * fine_rows, fine_rows) - row_id * coarse_rows
    cols = lax.dynamic_slice_in_dim(fine_map, col_id * fine_cols, fine_cols) - col_id * coarse_cols
    entries = jnp.arange(coefficient_table.shape[0], dtype=jnp.int32)
    table = jnp.where(entries > 0, coefficient_table, jnp.zeros_like(coefficient_table))
    edge = coefficient_index[:, fine_cols - 2 :, 1::2].transpose(0, 2, 1).reshape(-1)
    edge = jnp.sum(jnp.where(edge[:, None] == entries, table, jnp.zeros_like(table)), axis=-1)
    (u,) = call(rotate_kernel, "rotate", "vv", [((n_pairs, vecs, nb), F32)], [], 4, 10**8, (trial_vectors, right_rotation))
    foreign = shifted(edge, "colk", 1)
    foreign_u = shifted(jnp.stack([u[n_pairs - 3], u[n_pairs - 1]]), "colk", 1)
    source = (rows[:, None] + jnp.arange(2, dtype=jnp.int32)[None, :]).reshape(-1)
    numbers = jnp.arange(2 * fine_rows, dtype=jnp.int32)
    ahead = (source[None, :] < source[:, None]) | (
        (source[None, :] == source[:, None]) & (numbers[None, :] < numbers[:, None])
    )
    place = jnp.sum(ahead.astype(jnp.int32), axis=1)
    order = jnp.sum(jnp.where(place[None, :] == numbers[:, None], numbers[None, :], 0), axis=1)
    coarse = jnp.arange(coarse_rows + 1, dtype=jnp.int32)
    start = jnp.sum((source[None, :] < coarse[:, None]).astype(jnp.int32), axis=1)
    g, splat = call(
        prepare_kernel,
        "prepare",
        "ssssv",
        [((2 * fine_rows, vecs, coarse_cols * nb), BF16), ((2 * fine_rows * n_pairs, 8, 2 * nb), BF16)],
        [],
        24,
        10**9,
        (coefficient_index.reshape(-1), table, cols, order, u),
    )
    tied = lax.optimization_barrier((blocks, g, splat, rows, cols, place, order, start))
    blocks, g, splat, rows, cols, place, order, start = tied
    rim_row = shifted(blocks[0], "rowk", -1)
    rim_col = shifted(blocks[:, 0], "colk", -1)

    block_buffer = pltpu.VMEM((coarse_rows, coarse_cols, nb, nb), BF16)
    main, tail = call(
        forward_kernel,
        "forward",
        "ssssvhhh",
        [((n_cols, vecs, own * nb), BF16), ((own, vecs, coarse_cols * nb), BF16)],
        [
            pltpu.VMEM((2 * fine_rows + 8, vecs, coarse_cols * nb), BF16),
            block_buffer,
            pltpu.VMEM((2 * fine_rows + 8, vecs, nb), BF16),
            pltpu.VMEM(left_rotation.shape, BF16),
            dma((CHUNKS,)),
            dma((CHUNKS,)),
            dma((1,)),
        ],
        52,
        10**9,
        (order, place, start, foreign, foreign_u, left_rotation, g, blocks),
    )
    (partial,) = call(
        rim_kernel,
        "rim",
        "vvvva",
        [((n_cols, vecs, own * nb), BF16)],
        [],
        8,
        10**8,
        (main, tail, rim_row, left_rotation[fine_rows - own :, 1], rim_col),
    )
    corner = shifted(rim_row[0:1], "colk", -1)

    parts, corner = lax.optimization_barrier((exchange(partial, "colk"), corner))
    piece = (vecs, own * nb)
    forward_image, copies = call(
        share_kernel, "share", "v", [(piece, BF16), ((n_cols, *piece), BF16)], [], 8, 10**6, (parts,)
    )
    row_image = exchange(copies, "colk")

    (terms,) = call(
        adjoint_kernel,
        "adjoint",
        "ssvvvvvvhh",
        [((vecs, fine_cols * nb), BF16)],
        [
            pltpu.VMEM((2 * fine_rows, vecs, nb), BF16),
            pltpu.VMEM((2 * fine_rows, coarse_cols + 1, vecs // 2, 2 * nb), BF16),
            pltpu.VMEM((2 * fine_rows * n_pairs, 8, 2 * nb), BF16),
            pltpu.VMEM((coarse_rows + 1, coarse_cols, nb, nb), BF16),
            pltpu.VMEM((coarse_rows + 1, nb, nb), BF16),
            dma((coarse_cols + 4,)),
        ],
        52,
        10**9,
        (rows, cols, row_image, rim_row, rim_col, corner, left_rotation, right_rotation, splat, blocks),
    )

    terms = terms.reshape(n_rows, vecs // n_rows, fine_cols * nb)
    adjoint_image = jnp.sum(exchange(terms, "rowk").astype(F32), axis=0).astype(BF16)
    return (forward_image, adjoint_image)


def solution(mesh):
    return jax.shard_map(
        body,
        mesh=mesh,
        in_specs=(
            P(("rowk", "colk"), None, None, None),
            P("rowk", None, None, None),
            P("colk", None, None, None),
            P(),
            P("rowk", "colk", None),
            P(),
            P(None, "colk"),
        ),
        out_specs=(P(None, ("rowk", "colk")), P("rowk", "colk")),
        check_vma=False,
    )
```

time: 143 us -> 141 us (0.986)
  blocking collectives: 42.6 us -> 24.6 us
  starting transfers between devices: 14.3 us -> 23.4 us
  waiting for transfers between devices: 34.1 us -> 41 us
    all_to_all x3 -> x2, blocking collectives: 42.6 us -> 24.6 us  [exchange(): return lax.all_to_all(value, axis, split_axis=0, concat_axis=0, tiled=True)]
    all_to_all x1 -> x2, starting transfers between devices: 5.72 us -> 11 us  [exchange(): return lax.all_to_all(value, axis, split_axis=0, concat_axis=0, tiled=True)]
    all_to_all x1 -> x2, waiting for transfers between devices: 34.1 us -> 38.2 us  [exchange(): return lax.all_to_all(value, axis, split_axis=0, concat_axis=0, tiled=True)]
    ppermute x4 -> x5, starting transfers between devices: 8.59 us -> 12.4 us  [shifted(): return lax.ppermute(value, axis, pairs)]
    ppermute x4 -> x5, waiting for transfers between devices: 0.01 us -> 2.83 us  [shifted(): return lax.ppermute(value, axis, pairs)]
    pallas_call x5 -> x6, Pallas kernels: 38.5 us -> 39.2 us  [call(): pl.pallas_call(kernel, out_shape=[jax.ShapeDtypeStruct(shape, kind) for s...]
    unnamed x17 -> x15, local copies, waits for them, and re-layouts: 6.68 us -> 6.65 us
  transfers between devices with their start and end apart: 6 -> 7, of which waited for: 1 -> 3; matrix products, arithmetic and copies ran while one was open for 3% -> 3% of each run, Pallas kernels for 16% -> 16%
where the time goes in v3:
time: 141 us
  waiting for transfers between devices  41 us (29%)
  Pallas kernels  39.2 us (28%)
  blocking collectives  24.6 us (17%)
  starting transfers between devices  23.4 us (17%)
  local copies, waits for them, and re-layouts  10.1 us (7%)
    pallas_call x6, Pallas kernels, call(): pl.pallas_call(kernel, out_shape=[jax.ShapeDtypeStruct(shape, kind) for s...  39.2 us
    all_to_all x2, waiting for transfers between devices, exchange(): return lax.all_to_all(value, axis, split_axis=0, concat_axis=0, tiled=True)  38.2 us
    all_to_all x2, blocking collectives, exchange(): return lax.all_to_all(value, axis, split_axis=0, concat_axis=0, tiled=True)  24.6 us
    ppermute x5, starting transfers between devices, shifted(): return lax.ppermute(value, axis, pairs)  12.4 us
    all_to_all x2, starting transfers between devices, exchange(): return lax.all_to_all(value, axis, split_axis=0, concat_axis=0, tiled=True)  11 us
    unnamed x15, local copies, waits for them, and re-layouts  6.65 us
    ppermute x5, waiting for transfers between devices, shifted(): return lax.ppermute(value, axis, pairs)  2.83 us
  transfers between devices with their start and end apart: 7, of which 3 were waited for; matrix products, arithmetic and copies ran while one was open for 3% of the time, Pallas kernels for 16%

profile of v3, /device:TPU:0, one launch (start us, length us, event | category | flops | bytes accessed | tf_op | source)
XLA Modules:
  0.0 140.6 jit_solution(12166636580930205216)
XLA Ops:
  0.6 0.0 copy-start.4
  0.6 0.0 copy-start.6
  0.7 0.0 copy-start.2
  0.7 0.0 copy-start.3
  0.7 0.0 copy-start.5
  0.7 5.7 %all-to-all-start = ((bf16[16,8,128,128]{3,2,1,0:T(8,128)(2,1)}), bf16[16,8,128,128]{3,2,1,0:T(8,128)(2,1)}, u32[]{:S(2)}, u32[]{:S(2)}) async-start(bf16[16,8,128,128]{3,2,1,0:T(8,128)(2,1)} %bitcast.12), calls=%async_computation | async-start | bytes 8388608 | tf_op jit(solution)/shard_map/all_to_all | solution.py:314
  6.4 0.0 copy-done.4
  6.5 0.1 copy.15
  6.6 0.1 eq.17
  6.7 0.0 copy-done.6
  6.7 0.1 select_reduce_fusion.1
  6.8 0.4 collective-permute-start
  7.2 0.0 copy-done.3
  7.2 0.8 rotate.1.u_ref
  8.0 1.7 %collective-permute-start.1 = (f32[2,64,128]{2,1,0:T(8,128)S(1)}, f32[2,64,128]{2,1,0:T(8,128)S(1)}, u32[]{:S(2)}, u32[]{:S(2)}) collective-permute-start(f32[2,64,128]{2,1,0:T(8,128)S(1)} %pad_maximum_fusion), channel_id=1, source_target_pairs={{0,1},{1,2},{2,3},{3,4},{4,5},{5,6},{6,7},{7,8},{8,9},{9,10},{10,1... | collective-permute-start | bytes 196616 | tf_op jit(solution)/shard_map/ppermute | solution.py:44
  9.7 0.2 copy.14
  9.9 0.2 reshape.44.index_ref
  10.1 0.1 dynamic-slice_subtract_fusion.rows_ref
  10.2 0.1 iota_add_fusion
  10.3 0.1 add.35
  10.4 0.1 dynamic-slice_subtract_fusion.1.cols_ref
  10.5 0.2 convert_reduce_fusion.place_ref
  10.6 0.1 select_reduce_fusion.order_ref
  10.8 11.5 %prepare.1 = (bf16[64,64,1024]{2,1,0:T(8,128)(2,1)S(1)}, bf16[2048,8,256]{2,1,0:T(8,128)(2,1)S(1)}) custom-call(s32[2048]{0:T(1024)S(1)} %reshape.44.index_ref, f32[16]{0:T(128)S(1)} %compare_select_fusion.table_ref, s32[16]{0:T(128)S(1)} %dynamic-slice_subtract_fusion.1.cols_ref, s32[64]{0:T(128)S(1)} %select_reduce_fusion.order_ref, ...), custom_call_target="tpu_custom_call" | custom-call | flops 1000000000 | bytes 1057152 | tf_op jit(solution)/shard_map/prepare/pallas_call | solution.py:320
  22.3 3.2 %copy-done = bf16[2048,8,256]{2,1,0:T(8,128)(2,1)} copy-done((bf16[2048,8,256]{2,1,0:T(8,128)(2,1)}, bf16[2048,8,256]{2,1,0:T(8,128)(2,1)S(1)}, u32[]{:S(2)}) %copy-start) | copy-done | bytes 8388632
  25.5 3.2 %copy-done.1 = bf16[64,64,1024]{2,1,0:T(8,128)(2,1)} copy-done((bf16[64,64,1024]{2,1,0:T(8,128)(2,1)}, bf16[64,64,1024]{2,1,0:T(8,128)(2,1)S(1)}, u32[]{:S(2)}) %copy-start.1) | copy-done | bytes 8388632
  28.7 0.1 convert_reduce_fusion.1.start_ref
  28.8 34.0 %all-to-all-done.blocks_any = bf16[16,8,128,128]{3,2,1,0:T(8,128)(2,1)} async-done(((bf16[16,8,128,128]{3,2,1,0:T(8,128)(2,1)}), bf16[16,8,128,128]{3,2,1,0:T(8,128)(2,1)}, u32[]{:S(2)}, u32[]{:S(2)}) %all-to-all-start) | async-done | bytes 4194336 | tf_op jit(solution)/shard_map/all_to_all | solution.py:314
  62.9 1.1 slice_bitcast_fusion
  64.0 0.1 collective-permute-start.3
  64.0 1.0 slice_bitcast_fusion.1
  65.0 6.4 %collective-permute-start.2 = (bf16[8,128,128]{2,1,0:T(8,128)(2,1)S(1)}, bf16[8,128,128]{2,1,0:T(8,128)(2,1)S(1)}, u32[]{:S(2)}, u32[]{:S(2)}) collective-permute-start(bf16[8,128,128]{2,1,0:T(8,128)(2,1)S(1)} %slice_bitcast_fusion.1), channel_id=1, source_target_pairs={{0,112},{16,0},{32,16},{48,32},{64,48},{80,64},{96,80},{112,96},{1... | collective-permute-start | bytes 786440 | tf_op jit(solution)/shard_map/ppermute | solution.py:44
  71.5 0.8 slice_bitcast_fusion.2.left_ref
  72.3 0.0 collective-permute-done.foreign_ref
  72.3 0.0 collective-permute-done.1.foreign_u_ref
  72.3 9.9 %forward.1 = (bf16[16,64,256]{2,1,0:T(8,128)(2,1)S(1)}, bf16[2,64,1024]{2,1,0:T(8,128)(2,1)S(1)}) custom-call(s32[64]{0:T(128)S(1)} %select_reduce_fusion.order_ref, s32[64]{0:T(128)S(1)} %convert_reduce_fusion.place_ref, s32[17]{0:T(128)S(1)} %convert_reduce_fusion.1.start_ref, f32[128]{0:T(128)S(1)} %collective-permute-done.foreign_ref, ...), custom_call_target="tpu_custom_call" | custom-call | flops 1000000000 | bytes 14746692 | tf_op jit(solution)/shard_map/forward/pallas_call | solution.py:320
  82.2 0.0 collective-permute-done.2.rim_row_ref
  82.2 0.0 collective-permute-done.3.col_any.rim_col_ref
  82.2 1.5 %rim.1 = bf16[16,64,256]{2,1,0:T(8,128)(2,1)} custom-call(bf16[16,64,256]{2,1,0:T(8,128)(2,1)S(1)} %get-tuple-element.25.main_ref, bf16[2,64,1024]{2,1,0:T(8,128)(2,1)S(1)} %get-tuple-element.26.tail_ref, bf16[8,128,128]{2,1,0:T(8,128)(2,1)S(1)} %collective-permute-done.2.rim_row_ref, bf16[2,128,128]{2,1,0:T(8,128)(2,1)S(1)} %slice_bitcast_fusion.2.left_ref, ...), custom_call_target="tpu_custom_call" | custom-call | flops 100000000 | bytes 1638400 | tf_op jit(solution)/shard_map/rim/pallas_call | solution.py:320
  83.7 5.3 %all-to-all-start.1 = ((bf16[16,64,256]{2,1,0:T(8,128)(2,1)}), bf16[16,64,256]{2,1,0:T(8,128)(2,1)S(1)}, u32[]{:S(2)}, u32[]{:S(2)}) async-start(bf16[16,64,256]{2,1,0:T(8,128)(2,1)} %rim.1), calls=%async_computation.1 | async-start | bytes 1048576 | tf_op jit(solution)/shard_map/all_to_all | solution.py:314
  89.0 3.8 %collective-permute-start.4 = (bf16[1,128,128]{2,1,0:T(8,128)(2,1)S(1)}, bf16[1,128,128]{2,1,0:T(8,128)(2,1)S(1)}, u32[]{:S(2)}, u32[]{:S(2)}) collective-permute-start(bf16[1,128,128]{2,1,0:T(8,128)(2,1)S(1)} %slice.30), channel_id=1, source_target_pairs={{0,15},{1,0},{2,1},{3,2},{4,3},{5,4},{6,5},{7,6},{8,7},{9,8},{10,9... | collective-permute-start | bytes 98312 | tf_op jit(solution)/shard_map/ppermute | solution.py:44
  92.8 2.8 %collective-permute-done.4.corner_ref = bf16[1,128,128]{2,1,0:T(8,128)(2,1)S(1)} collective-permute-done((bf16[1,128,128]{2,1,0:T(8,128)(2,1)S(1)}, bf16[1,128,128]{2,1,0:T(8,128)(2,1)S(1)}, u32[]{:S(2)}, u32[]{:S(2)}) %collective-permute-start.4) | collective-permute-done | bytes 32800 | tf_op jit(solution)/shard_map/ppermute | solution.py:44
  95.6 4.2 %all-to-all-done.1.parts_ref = bf16[16,64,256]{2,1,0:T(8,128)(2,1)S(1)} async-done(((bf16[16,64,256]{2,1,0:T(8,128)(2,1)}), bf16[16,64,256]{2,1,0:T(8,128)(2,1)S(1)}, u32[]{:S(2)}, u32[]{:S(2)}) %all-to-all-start.1) | async-done | bytes 524320 | tf_op jit(solution)/shard_map/all_to_all | solution.py:314
  99.8 0.7 share.1
  100.5 13.4 %all_to_all.20.y_ref = bf16[16,64,256]{2,1,0:T(8,128)(2,1)S(1)} all-to-all(bf16[16,64,256]{2,1,0:T(8,128)(2,1)S(1)} %get-tuple-element.31), channel_id=1, replica_groups=mesh['rowk'=8,'colk'=16] {'colk'}, dimensions={0} | all-to-all | bytes 1048576 | tf_op jit(solution)/shard_map/all_to_all | solution.py:314
  114.0 14.8 %adjoint.1 = bf16[64,2048]{1,0:T(8,128)(2,1)S(1)} custom-call(s32[32]{0:T(128)S(1)} %dynamic-slice_subtract_fusion.rows_ref, s32[16]{0:T(128)S(1)} %dynamic-slice_subtract_fusion.1.cols_ref, bf16[16,64,256]{2,1,0:T(8,128)(2,1)S(1)} %all_to_all.20.y_ref, bf16[8,128,128]{2,1,0:T(8,128)(2,1)S(1)} %collective-permute-done.2.rim_row_ref, ...), custom_call_target="tpu_custom_call" | custom-call | flops 1000000000 | bytes 17072320 | tf_op jit(solution)/shard_map/adjoint/pallas_call | solution.py:320
  128.8 11.1 %all_to_all.21 = bf16[8,8,2048]{2,1,0:T(8,128)(2,1)S(1)} all-to-all(bf16[8,8,2048]{2,1,0:T(8,128)(2,1)S(1)} %bitcast.11), channel_id=1, replica_groups=mesh['rowk'=8,'colk'=16] {'rowk'}, dimensions={0} | all-to-all | bytes 524288 | tf_op jit(solution)/shard_map/all_to_all | solution.py:314
  140.0 0.7 reduce_sum.52
  (9 shorter events, 0.1 us)
Async XLA Ops:
  0.6 5.8 %copy-start.4 = (s32[32,16,4]{0,2,1:T(4,128)S(1)}, s32[32,16,4]{0,2,1:T(4,128)}, u32[]{:S(2)}) copy-start(s32[32,16,4]{0,2,1:T(4,128)} %param.11) | copy-start | bytes 24580
  0.6 6.1 %copy-start.6 = (f32[16]{0:T(128)S(1)}, f32[16]{0:T(128)}, u32[]{:S(2)}) copy-start(f32[16]{0:T(128)} %param.12) | copy-start | bytes 196
  0.7 6.5 %copy-start.2 = (bf16[16,2,128,128]{3,2,1,0:T(8,128)(2,1)S(1)}, bf16[16,2,128,128]{3,2,1,0:T(8,128)(2,1)}, u32[]{:S(2)}) copy-start(bf16[16,2,128,128]{3,2,1,0:T(8,128)(2,1)} %right_ref.3) | copy-start | bytes 3145732
  0.7 6.5 %copy-start.3 = (bf16[64,2048]{1,0:T(8,128)(2,1)S(1)}, bf16[64,2048]{1,0:T(8,128)(2,1)}, u32[]{:S(2)}) copy-start(bf16[64,2048]{1,0:T(8,128)(2,1)} %x_ref.1) | copy-start | bytes 786436
  0.7 9.4 %copy-start.5 = (s32[256]{0:T(256)S(1)}, s32[256]{0:T(256)}, u32[]{:S(2)}) copy-start(s32[256]{0:T(256)} %param.10) | copy-start | bytes 3076
  0.7 62.2 %all-to-all-start = ((bf16[16,8,128,128]{3,2,1,0:T(8,128)(2,1)}), bf16[16,8,128,128]{3,2,1,0:T(8,128)(2,1)}, u32[]{:S(2)}, u32[]{:S(2)}) async-start(bf16[16,8,128,128]{3,2,1,0:T(8,128)(2,1)} %bitcast.12), calls=%async_computation | async-start | bytes 8388608 | tf_op jit(solution)/shard_map/all_to_all | solution.py:314
  6.8 65.5 %collective-permute-start = (f32[128]{0:T(128)S(1)}, f32[128]{0:T(128)S(1)}, u32[]{:S(2)}, u32[]{:S(2)}) collective-permute-start(f32[128]{0:T(128)S(1)} %select_reduce_fusion.1), channel_id=1, source_target_pairs={{0,1},{1,2},{2,3},{3,4},{4,5},{5,6},{6,7},{7,8},{8,9},{9,10},{10,1... | collective-permute-start | bytes 1544 | tf_op jit(solution)/shard_map/ppermute | solution.py:44
  8.0 64.3 %collective-permute-start.1 = (f32[2,64,128]{2,1,0:T(8,128)S(1)}, f32[2,64,128]{2,1,0:T(8,128)S(1)}, u32[]{:S(2)}, u32[]{:S(2)}) collective-permute-start(f32[2,64,128]{2,1,0:T(8,128)S(1)} %pad_maximum_fusion), channel_id=1, source_target_pairs={{0,1},{1,2},{2,3},{3,4},{4,5},{5,6},{6,7},{7,8},{8,9},{9,10},{10,1... | collective-permute-start | bytes 196616 | tf_op jit(solution)/shard_map/ppermute | solution.py:44
  22.3 3.2 %copy-start = (bf16[2048,8,256]{2,1,0:T(8,128)(2,1)}, bf16[2048,8,256]{2,1,0:T(8,128)(2,1)S(1)}, u32[]{:S(2)}) copy-start(bf16[2048,8,256]{2,1,0:T(8,128)(2,1)S(1)} %get-tuple-element.33.splat_any) | copy-start | bytes 25165828
  25.5 3.2 %copy-start.1 = (bf16[64,64,1024]{2,1,0:T(8,128)(2,1)}, bf16[64,64,1024]{2,1,0:T(8,128)(2,1)S(1)}, u32[]{:S(2)}) copy-start(bf16[64,64,1024]{2,1,0:T(8,128)(2,1)S(1)} %get-tuple-element.23.g_any) | copy-start | bytes 25165828
  64.0 18.3 %collective-permute-start.3 = (bf16[16,128,128]{2,1,0:T(8,128)(2,1)S(1)}, bf16[16,128,128]{2,1,0:T(8,128)(2,1)S(1)}, u32[]{:S(2)}, u32[]{:S(2)}) collective-permute-start(bf16[16,128,128]{2,1,0:T(8,128)(2,1)S(1)} %slice_bitcast_fusion), channel_id=1, source_target_pairs={{0,15},{1,0},{2,1},{3,2},{4,3},{5,4},{6,5},{7,6},{8,7},{9,8},{10,9... | collective-permute-start | bytes 1572872 | tf_op jit(solution)/shard_map/ppermute | solution.py:44
  65.0 17.2 %collective-permute-start.2 = (bf16[8,128,128]{2,1,0:T(8,128)(2,1)S(1)}, bf16[8,128,128]{2,1,0:T(8,128)(2,1)S(1)}, u32[]{:S(2)}, u32[]{:S(2)}) collective-permute-start(bf16[8,128,128]{2,1,0:T(8,128)(2,1)S(1)} %slice_bitcast_fusion.1), channel_id=1, source_target_pairs={{0,112},{16,0},{32,16},{48,32},{64,48},{80,64},{96,80},{112,96},{1... | collective-permute-start | bytes 786440 | tf_op jit(solution)/shard_map/ppermute | solution.py:44
  83.7 16.1 %all-to-all-start.1 = ((bf16[16,64,256]{2,1,0:T(8,128)(2,1)}), bf16[16,64,256]{2,1,0:T(8,128)(2,1)S(1)}, u32[]{:S(2)}, u32[]{:S(2)}) async-start(bf16[16,64,256]{2,1,0:T(8,128)(2,1)} %rim.1), calls=%async_computation.1 | async-start | bytes 1048576 | tf_op jit(solution)/shard_map/all_to_all | solution.py:314
  89.0 6.6 %collective-permute-start.4 = (bf16[1,128,128]{2,1,0:T(8,128)(2,1)S(1)}, bf16[1,128,128]{2,1,0:T(8,128)(2,1)S(1)}, u32[]{:S(2)}, u32[]{:S(2)}) collective-permute-start(bf16[1,128,128]{2,1,0:T(8,128)(2,1)S(1)} %slice.30), channel_id=1, source_target_pairs={{0,15},{1,0},{2,1},{3,2},{4,3},{5,4},{6,5},{7,6},{8,7},{9,8},{10,9... | collective-permute-start | bytes 98312 | tf_op jit(solution)/shard_map/ppermute | solution.py:44
